TPU v7x, 32 devices: a whole 2x2x4 slice. The times are simulated.
32 devices in a mesh: pipe: 4 (over y, x), row: 2 (over core), col: 4 (over z).
Axes of the slice: x: 2, y: 2, z: 4, core: 2. Of those that a mesh axis runs over, the one named last changes fastest.
Arguments:
- act_handoff: bfloat16 [4, 512, 4096], P('pipe', 'col', 'row'), may hold values from -6 to 6
- grad_handoff: bfloat16 [4, 512, 4096], P('pipe', 'col', 'row'), may hold values from -6 to 6
- up_blocks: bfloat16 [4, 2, 4, 1024, 4096], P('pipe', 'row', 'col'), may hold values from -0.125 to 0.125
- down_blocks: bfloat16 [4, 2, 4, 1024, 4096], P('pipe', 'row', 'col'), may hold values from -0.0625 to 0.0625
- up_mask: int32 [4, 64, 224], P('pipe', 'row', 'col'), may hold values from 0 to 1, as said below
- down_mask: int32 [4, 224, 64], P('pipe', 'col', 'row'), may hold values from 0 to 1, as said below
Outputs:
- section_output: bfloat16 [4, 512, 4096], P('pipe', 'col', 'row')
- input_grad: bfloat16 [4, 512, 4096], P('pipe', 'col', 'row')
- up_grad: bfloat16 [4, 2, 4, 1024, 4096], P('pipe', 'row', 'col')
- down_grad: bfloat16 [4, 2, 4, 1024, 4096], P('pipe', 'row', 'col')
Inputs may be any that keep to these rules, and one draw needn't show every extreme that they name: `up_mask`: per section, every tile of either mask holds at most 1024 live blocks and at least 560, and in every section some tile holds exactly 1024. `down_mask`: as for up_mask, with tiles of 56 x 32 blocks.
All inputs are finite; a program needn't handle non-finite values.
Results may differ from a plain program's by a relative error of at most 0.013.
Values may be sent and summed in bfloat16 or wider, within the bound.
No kernel may reach another device: no remote copies, remote signals or barrier semaphores. Data moves between devices by JAX's collectives and lax.ppermute only.
A program may use at most 256 MiB of HBM per device.

v0:
```python
import functools
import jax
import jax.numpy as jnp
from jax import lax
from jax.experimental import pallas as pl
from jax.experimental.pallas import tpu as pltpu
from jax.sharding import PartitionSpec as P

BLK = 64
LANES = 128
PADROWS = 9


def low_half(rows):
    return lax.broadcasted_iota(jnp.int32, (rows, LANES), 1) < BLK


def largest_part(total, most):
    return max(part for part in range(1, most + 1) if total % part == 0)


def unpack_kernel(slot_ref, packed_ref, out_ref, raw_ref, stage_ref, sems, *, cols, capacity, group):
    pitch = capacity + PADROWS
    half = BLK // 2
    part = pl.program_id(0)
    step = pl.program_id(1)
    pieces = sems.shape[1]
    piece = capacity // pieces
    chunk = 64

    def fetch(h, p):
        return pltpu.make_async_copy(
            packed_ref.at[pl.ds(p * piece, piece), pl.ds(h * half * BLK, half * BLK)],
            raw_ref.at[h, pl.ds(p * piece, piece), :], sems.at[h, p])

    @pl.when((part == 0) & (step == 0))
    def _():
        for h in range(2):
            for p in range(pieces):
                fetch(h, p).start()
        for i in range(half):
            stage_ref[pl.ds(i * pitch + capacity, 8), :] = jnp.zeros((8, LANES), jnp.float32)

    def stage_half(h):
        keep = low_half(chunk)

        def stage(at, carry):
            base = pl.multiple_of(at * chunk, chunk)
            for tile in range(half // 2):
                value = raw_ref[h, pl.ds(base, chunk), tile * LANES:(tile + 1) * LANES].astype(jnp.float32)
                swapped = pltpu.roll(value, BLK, 1)
                stage_ref[pl.ds(2 * tile * pitch + base, chunk), :] = jnp.where(keep, value, swapped)
                stage_ref[pl.ds((2 * tile + 1) * pitch + base, chunk), :] = jnp.where(keep, swapped, value)
            return carry

        for p in range(pieces):
            fetch(h, p).wait()
            lax.fori_loop(p * piece // chunk, (p + 1) * piece // chunk, stage, 0)

    for h in range(2):
        pl.when((part == h) & (step == 0))(functools.partial(stage_half, h))

    keep = low_half(half)

    def block_row(r, carry):
        at = (step * group + r) * cols
        for pair in range(cols // 2):
            left = stage_ref[pl.ds(slot_ref[at + 2 * pair], half, stride=pitch), :]
            right = stage_ref[pl.ds(slot_ref[at + 2 * pair + 1], half, stride=pitch), :]
            out_ref[r, 0, :, pair * LANES:(pair + 1) * LANES] = jnp.where(keep, left, right).astype(jnp.bfloat16)
        return carry

    lax.fori_loop(0, group, block_row, 0)


def unpack(packed, slots, rows, cols):
    capacity = packed.shape[0]
    pitch = capacity + PADROWS
    half = BLK // 2
    group = largest_part(rows, 8)
    dense = pl.pallas_call(
        functools.partial(unpack_kernel, cols=cols, capacity=capacity, group=group),
        out_shape=jax.ShapeDtypeStruct((rows, 2, half, cols * BLK), jnp.bfloat16),
        grid_spec=pltpu.PrefetchScalarGridSpec(
            num_scalar_prefetch=1,
            grid=(2, rows // group),
            in_specs=[pl.BlockSpec(memory_space=pl.ANY)],
            out_specs=pl.BlockSpec((group, 1, half, cols * BLK), lambda h, r, s: (r, h, 0, 0)),
            scratch_shapes=[
                pltpu.VMEM((2, capacity, half * BLK), jnp.bfloat16),
                pltpu.VMEM((half * pitch, LANES), jnp.float32),
                pltpu.SemaphoreType.DMA((2, 4)),
            ],
        ),
        compiler_params=pltpu.CompilerParams(
            dimension_semantics=("arbitrary", "arbitrary"), vmem_limit_bytes=60 << 20
        ),
        name="unpack_tile",
    )(slots, packed)
    return dense.reshape(rows * BLK, cols * BLK)


def grad_kernel(slot_ref, count_ref, lhs_ref, rhs_ref, out_ref, turned_ref, even_ref, odd_ref, stage_ref, *,
                group, groups, cols, capacity, width, pairs, chunks):
    pitch = capacity + PADROWS
    half = BLK // 2
    step = pl.program_id(0)
    keep = low_half(half)

    def multiply(n, res_ref):
        base = pl.multiple_of(n * (pairs * LANES), pairs * LANES)
        value = jnp.dot(turned_ref[...], rhs_ref[:, pl.ds(base, pairs * LANES)], preferred_element_type=jnp.float32)
        for q in range(pairs):
            res_ref[q] = value[:, q * LANES:(q + 1) * LANES]

    def scatter(at, res_ref):
        valid = at >= 0
        at = jnp.maximum(at, 0)
        block_row = at // chunks * group
        block_col = at % chunks * (2 * pairs)
        for r in range(group):
            for q in range(pairs):
                even = res_ref[q, pl.ds(r * BLK, half, stride=2), :]
                odd = res_ref[q, pl.ds(r * BLK + 1, half, stride=2), :]
                first = jnp.where(keep, even, pltpu.roll(odd, BLK, 1))
                second = jnp.where(keep, pltpu.roll(even, BLK, 1), odd)
                where = (block_row + r) * cols + block_col + 2 * q
                one = jnp.where(valid, slot_ref[where], capacity)
                two = jnp.where(valid, slot_ref[where + 1], capacity)
                stage_ref[pl.ds(one, half, stride=pitch), :] = first
                stage_ref[pl.ds(two, half, stride=pitch), :] = second

    @pl.when(step < groups)
    def _():
        turned_ref[...] = lhs_ref[...].T
        if chunks % 2:
            def one_chunk(n, carry):
                multiply(n, even_ref)
                scatter(step * chunks + n, even_ref)
                return carry

            lax.fori_loop(0, chunks, one_chunk, 0)
        else:
            def two_chunks(m, carry):
                at = step * chunks + 2 * m
                multiply(2 * m, even_ref)
                scatter(at - 1, odd_ref)
                multiply(2 * m + 1, odd_ref)
                scatter(at, even_ref)
                return carry

            lax.fori_loop(0, chunks // 2, two_chunks, 0)

    if chunks % 2 == 0:
        @pl.when(step == groups)
        def _():
            scatter(groups * chunks - 1, odd_ref)

    @pl.when(step >= groups)
    def _():
        count = count_ref[0]
        chunk = 64
        tiles = width // LANES
        first_tile = (step - groups) * tiles

        def emit(s, carry):
            base = pl.multiple_of(s * chunk, chunk)
            live = lax.broadcasted_iota(jnp.int32, (chunk, LANES), 0) + base < count
            for t in range(tiles):
                value = stage_ref[pl.ds((first_tile + t) * pitch + base, chunk), :]
                out_ref[pl.ds(base, chunk), t * LANES:(t + 1) * LANES] = jnp.where(live, value, 0.0).astype(jnp.bfloat16)
            return carry

        lax.fori_loop(0, capacity // chunk, emit, 0)


def packed_grad(lhs, rhs, slots, count, rows, cols, capacity):
    tokens = lhs.shape[0]
    pitch = capacity + PADROWS
    half = BLK // 2
    group = max(g for g in range(1, 9) if rows % g == 0 and g * BLK % LANES == 0 or g == rows)
    groups = rows // group
    pairs = 2 if cols % 4 == 0 else 1
    width = 1024
    span = group * BLK
    emits = BLK * BLK // width
    return pl.pallas_call(
        functools.partial(grad_kernel, group=group, groups=groups, cols=cols, capacity=capacity, width=width,
                          pairs=pairs, chunks=cols // (2 * pairs)),
        out_shape=jax.ShapeDtypeStruct((capacity, BLK * BLK), jnp.bfloat16),
        grid_spec=pltpu.PrefetchScalarGridSpec(
            num_scalar_prefetch=2,
            grid=(groups + emits,),
            in_specs=[
                pl.BlockSpec((tokens, span), lambda s, a, b: (0, jnp.minimum(s, groups - 1))),
                pl.BlockSpec((tokens, cols * BLK), lambda s, a, b: (0, 0)),
            ],
            out_specs=pl.BlockSpec((capacity, width), lambda s, a, b: (0, jnp.maximum(s - groups, 0))),
            scratch_shapes=[
                pltpu.VMEM((span, tokens), jnp.bfloat16),
                pltpu.VMEM((pairs, span, LANES), jnp.float32),
                pltpu.VMEM((pairs, span, LANES), jnp.float32),
                pltpu.VMEM((half * pitch, LANES), jnp.float32),
            ],
        ),
        compiler_params=pltpu.CompilerParams(
            dimension_semantics=("arbitrary",), vmem_limit_bytes=50 << 20
        ),
        name="packed_grad",
    )(slots, count, lhs, rhs)


def moved(value, axis, pairs):
    return lax.ppermute(value, axis, pairs)


def shifted(value, axis, steps):
    count = lax.axis_size(axis)
    return moved(value, axis, [(source, (source + steps) % count) for source in range(count)])


def row_others(part):
    return [shifted(part, "row", steps) for steps in range(1, lax.axis_size("row"))]


def wide_sum(parts):
    total = parts[0].astype(jnp.float32)
    for part in parts[1:]:
        total = total + part.astype(jnp.float32)
    return total


def slope_of(value):
    sigma = jax.nn.sigmoid(value)
    return sigma * (1.0 + value * (1.0 - sigma))


def slots_of(grid, capacity):
    live = grid.reshape(-1)
    slots = jnp.cumsum(live) - live
    return jnp.where(live > 0, slots, capacity).astype(jnp.int32), jnp.sum(live, keepdims=True)


def product(left, right, dims):
    return lax.dot_general(left, right, (dims, ((), ())), preferred_element_type=jnp.float32).astype(jnp.bfloat16)


UPWARD = [(0, 1), (1, 2), (2, 3)]
DOWNWARD = [(1, 0), (2, 1), (3, 2)]
OUTWARD = [(1, 0), (2, 3)]


def after(value, *earlier):
    return lax.optimization_barrier((value, *earlier))[0]


def direct_scatter(part):
    count = lax.axis_size("col")
    rows = part.shape[0] // count
    own = part[:rows]
    return [own] + [shifted(part[d * rows:(d + 1) * rows], "col", d) for d in range(1, count)]


def direct_gather(value):
    others = [shifted(value, "col", -d) for d in range(1, lax.axis_size("col"))]
    return jnp.concatenate([value] + others, axis=0)


def near_gather(value, waits):
    if lax.axis_size("col") != 4:
        return direct_gather(value)
    place = lax.axis_index("col")
    opposite = shifted(value, "col", 2)
    above = moved(value, "col", DOWNWARD)
    below = moved(value, "col", UPWARD)
    far = moved(after(opposite, *waits), "col", OUTWARD)
    return jnp.concatenate(
        [value, jnp.where(place == 3, far, above), opposite, jnp.where(place == 0, far, below)], axis=0)


def body(act_handoff, grad_handoff, up_blocks, down_blocks, up_mask, down_mask):
    capacity = up_blocks.shape[3]
    rows, cols = up_mask.shape[1:]
    up_slots, up_count = slots_of(up_mask[0], capacity)
    down_slots, down_count = slots_of(down_mask[0], capacity)
    tok_in = shifted(act_handoff, "pipe", 1)
    grad_in = shifted(after(grad_handoff, tok_in), "pipe", -1)[0]
    tok_in = tok_in[0]
    up = unpack(up_blocks[0, 0, 0], after(up_slots, tok_in), rows, cols)
    tokens = near_gather(tok_in, (up,))
    down = unpack(down_blocks[0, 0, 0], after(down_slots, up), cols, rows)
    part = product(tokens, up, ((1,), (0,)))
    grads = near_gather(after(grad_in, tokens), (part,))
    pre = wide_sum([part] + row_others(part))
    hidden = jax.nn.silu(pre).astype(jnp.bfloat16)
    branch_part = product(hidden, down, ((1,), (0,)))
    branch = direct_scatter(branch_part)
    part = product(after(grads, branch_part), down, ((1,), (1,)))
    hidden_grad = wide_sum([part] + row_others(part))
    pre_grad = (hidden_grad * slope_of(pre)).astype(jnp.bfloat16)
    back_part = product(pre_grad, up, ((1,), (1,)))
    back = direct_scatter(back_part)
    down_grad = packed_grad(after(hidden, back_part), grads, down_slots, down_count, cols, rows, capacity)
    up_grad = packed_grad(after(tokens, down_grad), pre_grad, up_slots, up_count, rows, cols, capacity)
    section_output = wide_sum([tok_in] + branch).astype(jnp.bfloat16)[None]
    input_grad = wide_sum([grad_in] + back).astype(jnp.bfloat16)[None]
    return (section_output, input_grad, up_grad[None, None, None], down_grad[None, None, None])


def solution(mesh):
    return jax.shard_map(
        body,
        mesh=mesh,
        in_specs=(
            P("pipe", "col", "row"),
            P("pipe", "col", "row"),
            P("pipe", "row", "col", None, None),
            P("pipe", "row", "col", None, None),
            P("pipe", "row", "col"),
            P("pipe", "col", "row"),
        ),
        out_specs=(
            P("pipe", "col", "row"),
            P("pipe", "col", "row"),
            P("pipe", "row", "col", None, None),
            P("pipe", "row", "col", None, None),
        ),
        check_vma=False,
    )
```

profile of v0, /device:TPU:21, one launch (start us, length us, event | category | flops | bytes accessed | tf_op | source)
XLA Modules:
  0.0 292.2 jit_solution(8440060524279391057)
XLA Ops:
  0.6 1.3 collective-permute-start
  1.9 12.7 %collective-permute-done = bf16[1,128,2048]{2,1,0:T(8,128)(2,1)S(1)} collective-permute-done((bf16[1,128,2048]{2,1,0:T(8,128)(2,1)}, bf16[1,128,2048]{2,1,0:T(8,128)(2,1)S(1)}, u32[]{:S(2)}, u32[]{:S(2)}) %collective-permute-start) | collective-permute-done | bytes 524320 | tf_op jit(solution)/shard_map/ppermute | solution.py:214
  14.6 0.1 collective-permute-start.1
  14.7 0.8 reshape_squeeze.6
  15.5 0.8 reshape.44
  16.3 0.3 reduce-window.16
  16.5 0.1 slice.50
  16.7 0.1 slice_reduce_fusion.1
  16.8 0.7 fusion.3.slot_ref
  17.5 4.3 %collective-permute-start.3 = (bf16[128,2048]{1,0:T(8,128)(2,1)S(1)}, bf16[128,2048]{1,0:T(8,128)(2,1)S(1)}, u32[]{:S(2)}, u32[]{:S(2)}) collective-permute-start(bf16[128,2048]{1,0:T(8,128)(2,1)S(1)} %bitcast.40), channel_id=1, source_target_pairs={{1,0},{2,1},{3,2},{5,4},{6,5},{7,6},{9,8},{10,9},{11,10},{13,12},{... | collective-permute-start | bytes 1572872 | tf_op jit(solution)/shard_map/ppermute | solution.py:214
  21.8 1.9 collective-permute-start.4
  23.7 15.2 %unpack_tile.2 = bf16[32,2,32,3584]{3,2,1,0:T(8,128)(2,1)} custom-call(s32[1792]{0:T(1024)} %fusion.3.slot_ref, bf16[1024,4096]{1,0:T(8,128)(2,1)} %bitcast.35), custom_call_target="tpu_custom_call" | custom-call | tf_op jit(solution)/shard_map/unpack_tile/pallas_call | solution.py:81
  38.9 0.0 collective-permute-done.1
  38.9 0.0 copy-start.6
  38.9 4.8 %collective-permute-start.2 = (bf16[128,2048]{1,0:T(8,128)(2,1)S(1)}, bf16[128,2048]{1,0:T(8,128)(2,1)S(1)}, u32[]{:S(2)}, u32[]{:S(2)}) collective-permute-start(bf16[128,2048]{1,0:T(8,128)(2,1)S(1)} %collective-permute-done.1), channel_id=1, source_target_pairs={{1,0},{2,3},{5,4},{6,7},{9,8},{10,11},{13,12},{14,15},{17,16},{18,... | collective-permute-start | bytes 1572872 | tf_op jit(solution)/shard_map/ppermute | solution.py:214
  43.8 4.1 %collective-permute-done.3 = bf16[128,2048]{1,0:T(8,128)(2,1)S(1)} collective-permute-done((bf16[128,2048]{1,0:T(8,128)(2,1)S(1)}, bf16[128,2048]{1,0:T(8,128)(2,1)S(1)}, u32[]{:S(2)}, u32[]{:S(2)}) %collective-permute-start.3) | collective-permute-done | bytes 524320 | tf_op jit(solution)/shard_map/ppermute | solution.py:214
  47.8 4.1 %collective-permute-done.4 = bf16[128,2048]{1,0:T(8,128)(2,1)S(1)} collective-permute-done((bf16[128,2048]{1,0:T(8,128)(2,1)S(1)}, bf16[128,2048]{1,0:T(8,128)(2,1)S(1)}, u32[]{:S(2)}, u32[]{:S(2)}) %collective-permute-start.4) | collective-permute-done | bytes 524320 | tf_op jit(solution)/shard_map/ppermute | solution.py:214
  51.9 3.7 %collective-permute-done.2 = bf16[128,2048]{1,0:T(8,128)(2,1)S(1)} collective-permute-done((bf16[128,2048]{1,0:T(8,128)(2,1)S(1)}, bf16[128,2048]{1,0:T(8,128)(2,1)S(1)}, u32[]{:S(2)}, u32[]{:S(2)}) %collective-permute-start.2) | collective-permute-done | bytes 524320 | tf_op jit(solution)/shard_map/ppermute | solution.py:214
  55.5 0.1 broadcast_select_fusion.3
  55.6 0.0 copy-start.9
  55.6 12.3 %convolution_convert_fusion.1 = bf16[512,3584]{1,0:T(8,128)(2,1)} fusion(bf16[2048,3584]{1,0:T(8,128)(2,1)} %bitcast.31, bf16[128,2048]{1,0:T(8,128)(2,1)S(1)} %get-tuple-element.31, bf16[128,2048]{1,0:T(8,128)(2,1)S(1)} %collective-permute-done.1, bf16[128,2048]{1,0:T(8,128)(2,1)S(1)} %get-tuple-element.30, bf16[128,2048]{1,0:T(8,128)(2,1)S(1)} %bitcast.42), kind=kOutput, calls=%fused_computation.5 | convolution fusion | flops 7526416384 | bytes 20447232 | tf_op jit(solution)/shard_map/dot_general | solution.py:245
  67.9 2.7 collective-permute-start.5
  70.6 0.2 collective-permute-start.9
  70.9 1.2 pad_maximum_fusion.lhs_ref
  72.1 11.9 %collective-permute-done.9 = bf16[1,128,2048]{2,1,0:T(8,128)(2,1)S(1)} collective-permute-done((bf16[1,128,2048]{2,1,0:T(8,128)(2,1)S(1)}, bf16[1,128,2048]{2,1,0:T(8,128)(2,1)S(1)}, u32[]{:S(2)}, u32[]{:S(2)}) %collective-permute-start.9) | collective-permute-done | bytes 524320 | tf_op jit(solution)/shard_map/ppermute | solution.py:214
  84.0 0.0 collective-permute-start.10
  84.0 5.3 %collective-permute-start.12 = (bf16[128,2048]{1,0:T(8,128)(2,1)S(1)}, bf16[128,2048]{1,0:T(8,128)(2,1)}, u32[]{:S(2)}, u32[]{:S(2)}) collective-permute-start(bf16[128,2048]{1,0:T(8,128)(2,1)S(1)} %bitcast.45), channel_id=1, source_target_pairs={{1,0},{2,1},{3,2},{5,4},{6,5},{7,6},{9,8},{10,9},{11,10},{13,12},{... | collective-permute-start | bytes 1572872 | tf_op jit(solution)/shard_map/ppermute | solution.py:214
  89.3 1.9 collective-permute-start.13
  91.2 14.7 %collective-permute-done.10 = bf16[128,2048]{1,0:T(8,128)(2,1)} collective-permute-done((bf16[128,2048]{1,0:T(8,128)(2,1)S(1)}, bf16[128,2048]{1,0:T(8,128)(2,1)}, u32[]{:S(2)}, u32[]{:S(2)}) %collective-permute-start.10) | collective-permute-done | bytes 524320 | tf_op jit(solution)/shard_map/ppermute | solution.py:214
  105.9 8.1 %collective-permute-start.11 = (bf16[128,2048]{1,0:T(8,128)(2,1)}, bf16[128,2048]{1,0:T(8,128)(2,1)}, u32[]{:S(2)}, u32[]{:S(2)}) collective-permute-start(bf16[128,2048]{1,0:T(8,128)(2,1)} %collective-permute-done.10), channel_id=1, source_target_pairs={{1,0},{2,3},{5,4},{6,7},{9,8},{10,11},{13,12},{14,15},{17,16},{18,... | collective-permute-start | bytes 1572872 | tf_op jit(solution)/shard_map/ppermute | solution.py:214
  114.0 0.1 copy.10
  114.1 0.1 reshape_squeeze.7
  114.2 0.1 reshape.47
  114.3 0.3 reduce-window.24
  114.6 0.1 slice.52
  114.7 0.1 slice_reduce_fusion
  114.8 0.7 fusion.2.slot_ref
  115.5 16.8 %unpack_tile.3 = bf16[56,2,32,2048]{3,2,1,0:T(8,128)(2,1)} custom-call(s32[1792]{0:T(1024)} %fusion.2.slot_ref, bf16[1024,4096]{1,0:T(8,128)(2,1)} %bitcast.36), custom_call_target="tpu_custom_call" | custom-call | tf_op jit(solution)/shard_map/unpack_tile/pallas_call | solution.py:81
  132.3 0.0 collective-permute-done.12
  132.3 1.5 broadcast_select_fusion.2
  133.7 1.2 pad_maximum_fusion.1.rhs_ref
  134.9 4.9 %multiply_convert_fusion.1.lhs_ref = bf16[512,3584]{1,0:T(8,128)(2,1)S(1)} fusion(bf16[512,3584]{1,0:T(8,128)(2,1)} %collective-permute-done.5, bf16[512,3584]{1,0:T(8,128)(2,1)} %convolution_convert_fusion.1), kind=kLoop, calls=%fused_computation.1 | loop fusion | flops 14680064 | bytes 11010048 | tf_op jit(solution)/shard_map/convert_element_type | solution.py:295
  139.9 1.8 copy-done.4
  141.7 12.0 %convolution_convert_fusion.3 = bf16[512,2048]{1,0:T(8,128)(2,1)} fusion(bf16[512,3584]{1,0:T(8,128)(2,1)S(1)} %multiply_convert_fusion.1.lhs_ref, bf16[3584,2048]{1,0:T(8,128)(2,1)} %bitcast.33), kind=kOutput, calls=%fused_computation.7 | convolution fusion | flops 7517241344 | bytes 20447232 | tf_op jit(solution)/shard_map/dot_general | solution.py:245
  153.7 12.5 %convolution_convert_fusion = bf16[512,3584]{1,0:T(8,128)(2,1)} fusion(bf16[512,2048]{1,0:T(8,128)(2,1)S(1)} %pad_maximum_fusion.1.rhs_ref, bf16[3584,2048]{1,0:T(8,128)(2,1)} %bitcast.34), kind=kOutput, calls=%fused_computation.4 | convolution fusion | flops 7518027776 | bytes 20447232 | tf_op jit(solution)/shard_map/dot_general | solution.py:245
  166.2 0.9 collective-permute-start.14
  167.1 0.7 reduce_sum.18
  167.7 0.6 reduce_sum.19
  168.3 1.5 fusion.5
  169.8 0.2 collective-permute-start.8
  170.0 0.3 collective-permute-start.7
  170.3 1.1 collective-permute-start.6
  171.3 2.1 collective-permute-done.14
  173.5 7.1 %multiply_convert_fusion.rhs_ref = bf16[512,3584]{1,0:T(8,128)(2,1)S(1)} fusion(bf16[512,3584]{1,0:T(8,128)(2,1)} %collective-permute-done.14, bf16[512,3584]{1,0:T(8,128)(2,1)} %convolution_convert_fusion, bf16[512,3584]{1,0:T(8,128)(2,1)} %collective-permute-done.5, bf16[512,3584]{1,0:T(8,128)(2,1)} %convolution_convert_fusion.1), kind=kLoop, calls=%fused_computation | loop fusion | flops 27525120 | bytes 18350080 | tf_op jit(solution)/shard_map/convert_element_type | solution.py:300
  180.6 12.4 %convolution_convert_fusion.2 = bf16[512,2048]{1,0:T(8,128)(2,1)S(1)} fusion(bf16[512,3584]{1,0:T(8,128)(2,1)S(1)} %multiply_convert_fusion.rhs_ref, bf16[2048,3584]{1,0:T(8,128)(2,1)} %bitcast.32), kind=kOutput, calls=%fused_computation.6 | convolution fusion | flops 7517241344 | bytes 20447232 | tf_op jit(solution)/shard_map/dot_general | solution.py:245
  193.0 1.2 fusion.4
  194.2 0.1 collective-permute-start.17
  194.3 2.0 collective-permute-start.16
  196.3 18.7 %collective-permute-done.7 = bf16[128,2048]{1,0:T(8,128)(2,1)S(1)} collective-permute-done((bf16[128,2048]{1,0:T(8,128)(2,1)S(1)}, bf16[128,2048]{1,0:T(8,128)(2,1)S(1)}, u32[]{:S(2)}, u32[]{:S(2)}) %collective-permute-start.7) | collective-permute-done | bytes 524320 | tf_op jit(solution)/shard_map/ppermute | solution.py:214
  215.0 23.9 %collective-permute-done.6 = bf16[128,2048]{1,0:T(8,128)(2,1)S(1)} collective-permute-done((bf16[128,2048]{1,0:T(8,128)(2,1)S(1)}, bf16[128,2048]{1,0:T(8,128)(2,1)S(1)}, u32[]{:S(2)}, u32[]{:S(2)}) %collective-permute-start.6) | collective-permute-done | bytes 524320 | tf_op jit(solution)/shard_map/ppermute | solution.py:214
  238.9 2.3 fusion
  241.2 24.7 %packed_grad.2 = bf16[1024,4096]{1,0:T(8,128)(2,1)} custom-call(s32[1792]{0:T(1024)S(1)} %copy-done.3, s32[1]{0:T(128)} %bitcast.11.count_ref, bf16[512,3584]{1,0:T(8,128)(2,1)} %copy-done.4, bf16[512,2048]{1,0:T(8,128)(2,1)S(1)} %copy-done.1), custom_call_target="tpu_custom_call" | custom-call | tf_op jit(solution)/shard_map/packed_grad/pallas_call | solution.py:187
  265.9 25.1 %packed_grad.3 = bf16[1024,4096]{1,0:T(8,128)(2,1)} custom-call(s32[1792]{0:T(1024)S(1)} %copy-done.2, s32[1]{0:T(128)} %bitcast.10.count_ref, bf16[512,2048]{1,0:T(8,128)(2,1)S(1)} %pad_maximum_fusion.lhs_ref, bf16[512,3584]{1,0:T(8,128)(2,1)} %copy-done.5), custom_call_target="tpu_custom_call" | custom-call | tf_op jit(solution)/shard_map/packed_grad/pallas_call | solution.py:187
  290.9 1.2 fusion.1
  (27 shorter events, 0.1 us)
Async XLA Ops:
  0.6 14.0 %collective-permute-start = (bf16[1,128,2048]{2,1,0:T(8,128)(2,1)}, bf16[1,128,2048]{2,1,0:T(8,128)(2,1)S(1)}, u32[]{:S(2)}, u32[]{:S(2)}) collective-permute-start(bf16[1,128,2048]{2,1,0:T(8,128)(2,1)} %param.6), channel_id=1, source_target_pairs={{0,8},{8,16},{16,24},{24,0},{1,9},{9,17},{17,25},{25,1},{2,10},{10... | collective-permute-start | bytes 1572872 | tf_op jit(solution)/shard_map/ppermute | solution.py:214
  14.6 24.3 %collective-permute-start.1 = (bf16[128,2048]{1,0:T(8,128)(2,1)S(1)}, bf16[128,2048]{1,0:T(8,128)(2,1)S(1)}, u32[]{:S(2)}, u32[]{:S(2)}) collective-permute-start(bf16[128,2048]{1,0:T(8,128)(2,1)S(1)} %bitcast.39), channel_id=1, source_target_pairs={{0,2},{1,3},{2,0},{3,1},{4,6},{5,7},{6,4},{7,5},{8,10},{9,11},{10,... | collective-permute-start | bytes 1572872 | tf_op jit(solution)/shard_map/ppermute | solution.py:214
  17.5 30.4 %collective-permute-start.3 = (bf16[128,2048]{1,0:T(8,128)(2,1)S(1)}, bf16[128,2048]{1,0:T(8,128)(2,1)S(1)}, u32[]{:S(2)}, u32[]{:S(2)}) collective-permute-start(bf16[128,2048]{1,0:T(8,128)(2,1)S(1)} %bitcast.40), channel_id=1, source_target_pairs={{1,0},{2,1},{3,2},{5,4},{6,5},{7,6},{9,8},{10,9},{11,10},{13,12},{... | collective-permute-start | bytes 1572872 | tf_op jit(solution)/shard_map/ppermute | solution.py:214
  21.8 30.1 %collective-permute-start.4 = (bf16[128,2048]{1,0:T(8,128)(2,1)S(1)}, bf16[128,2048]{1,0:T(8,128)(2,1)S(1)}, u32[]{:S(2)}, u32[]{:S(2)}) collective-permute-start(bf16[128,2048]{1,0:T(8,128)(2,1)S(1)} %bitcast.41), channel_id=1, source_target_pairs={{0,1},{1,2},{2,3},{4,5},{5,6},{6,7},{8,9},{9,10},{10,11},{12,13},{... | collective-permute-start | bytes 1572872 | tf_op jit(solution)/shard_map/ppermute | solution.py:214
  38.9 29.0 %copy-start.6 = (bf16[128,2048]{1,0:T(8,128)(2,1)}, bf16[128,2048]{1,0:T(8,128)(2,1)S(1)}, u32[]{:S(2)}) copy-start(bf16[128,2048]{1,0:T(8,128)(2,1)S(1)} %collective-permute-done.1) | copy-start | bytes 1572868
  38.9 16.6 %collective-permute-start.2 = (bf16[128,2048]{1,0:T(8,128)(2,1)S(1)}, bf16[128,2048]{1,0:T(8,128)(2,1)S(1)}, u32[]{:S(2)}, u32[]{:S(2)}) collective-permute-start(bf16[128,2048]{1,0:T(8,128)(2,1)S(1)} %collective-permute-done.1), channel_id=1, source_target_pairs={{1,0},{2,3},{5,4},{6,7},{9,8},{10,11},{13,12},{14,15},{17,16},{18,... | collective-permute-start | bytes 1572872 | tf_op jit(solution)/shard_map/ppermute | solution.py:214
  55.6 15.0 %copy-start.9 = (bf16[1,128,2048]{2,1,0:T(8,128)(2,1)S(1)}, bf16[1,128,2048]{2,1,0:T(8,128)(2,1)}, u32[]{:S(2)}) copy-start(bf16[1,128,2048]{2,1,0:T(8,128)(2,1)} %param.7) | copy-start | bytes 1572868
  67.9 46.1 %copy-start.8 = (s32[1,56,32]{1,2,0:T(8,128)S(1)}, s32[1,56,32]{1,2,0:T(8,128)}, u32[]{:S(2)}) copy-start(s32[1,56,32]{1,2,0:T(8,128)} %param.11) | copy-start | bytes 21508
  67.9 67.0 %collective-permute-start.5 = (bf16[512,3584]{1,0:T(8,128)(2,1)}, bf16[512,3584]{1,0:T(8,128)(2,1)}, u32[]{:S(2)}, u32[]{:S(2)}) collective-permute-start(bf16[512,3584]{1,0:T(8,128)(2,1)} %convolution_convert_fusion.1), channel_id=1, source_target_pairs={{0,4},{4,0},{1,5},{5,1},{2,6},{6,2},{3,7},{7,3},{8,12},{12,8},{9,1... | collective-permute-start | bytes 11010056 | tf_op jit(solution)/shard_map/ppermute | solution.py:214
  70.6 13.4 %collective-permute-start.9 = (bf16[1,128,2048]{2,1,0:T(8,128)(2,1)S(1)}, bf16[1,128,2048]{2,1,0:T(8,128)(2,1)S(1)}, u32[]{:S(2)}, u32[]{:S(2)}) collective-permute-start(bf16[1,128,2048]{2,1,0:T(8,128)(2,1)S(1)} %copy-done.9), channel_id=1, source_target_pairs={{0,24},{8,0},{16,8},{24,16},{1,25},{9,1},{17,9},{25,17},{2,26},{10... | collective-permute-start | bytes 1572872 | tf_op jit(solution)/shard_map/ppermute | solution.py:214
  84.0 21.9 %collective-permute-start.10 = (bf16[128,2048]{1,0:T(8,128)(2,1)S(1)}, bf16[128,2048]{1,0:T(8,128)(2,1)}, u32[]{:S(2)}, u32[]{:S(2)}) collective-permute-start(bf16[128,2048]{1,0:T(8,128)(2,1)S(1)} %bitcast.44), channel_id=1, source_target_pairs={{0,2},{1,3},{2,0},{3,1},{4,6},{5,7},{6,4},{7,5},{8,10},{9,11},{10,... | collective-permute-start | bytes 1572872 | tf_op jit(solution)/shard_map/ppermute | solution.py:214
  84.0 48.2 %collective-permute-start.12 = (bf16[128,2048]{1,0:T(8,128)(2,1)S(1)}, bf16[128,2048]{1,0:T(8,128)(2,1)}, u32[]{:S(2)}, u32[]{:S(2)}) collective-permute-start(bf16[128,2048]{1,0:T(8,128)(2,1)S(1)} %bitcast.45), channel_id=1, source_target_pairs={{1,0},{2,1},{3,2},{5,4},{6,5},{7,6},{9,8},{10,9},{11,10},{13,12},{... | collective-permute-start | bytes 1572872 | tf_op jit(solution)/shard_map/ppermute | solution.py:214
  89.3 43.0 %collective-permute-start.13 = (bf16[128,2048]{1,0:T(8,128)(2,1)S(1)}, bf16[128,2048]{1,0:T(8,128)(2,1)}, u32[]{:S(2)}, u32[]{:S(2)}) collective-permute-start(bf16[128,2048]{1,0:T(8,128)(2,1)S(1)} %bitcast.46), channel_id=1, source_target_pairs={{0,1},{1,2},{2,3},{4,5},{5,6},{6,7},{8,9},{9,10},{10,11},{12,13},{... | collective-permute-start | bytes 1572872 | tf_op jit(solution)/shard_map/ppermute | solution.py:214
  105.9 26.3 %collective-permute-start.11 = (bf16[128,2048]{1,0:T(8,128)(2,1)}, bf16[128,2048]{1,0:T(8,128)(2,1)}, u32[]{:S(2)}, u32[]{:S(2)}) collective-permute-start(bf16[128,2048]{1,0:T(8,128)(2,1)} %collective-permute-done.10), channel_id=1, source_target_pairs={{1,0},{2,3},{5,4},{6,7},{9,8},{10,11},{13,12},{14,15},{17,16},{18,... | collective-permute-start | bytes 1572872 | tf_op jit(solution)/shard_map/ppermute | solution.py:214
  134.9 18.8 %copy-start = (bf16[512,2048]{1,0:T(8,128)(2,1)}, bf16[512,2048]{1,0:T(8,128)(2,1)S(1)}, u32[]{:S(2)}) copy-start(bf16[512,2048]{1,0:T(8,128)(2,1)S(1)} %pad_maximum_fusion.1.rhs_ref) | copy-start | bytes 6291460
  139.9 1.8 copy-start.4
  153.7 13.4 %copy-start.7 = (s32[1,32,56]{2,1,0:T(8,128)S(1)}, s32[1,32,56]{2,1,0:T(8,128)}, u32[]{:S(2)}) copy-start(s32[1,32,56]{2,1,0:T(8,128)} %param.10) | copy-start | bytes 21508
  166.2 7.2 %collective-permute-start.14 = (bf16[512,3584]{1,0:T(8,128)(2,1)}, bf16[512,3584]{1,0:T(8,128)(2,1)}, u32[]{:S(2)}, u32[]{:S(2)}) collective-permute-start(bf16[512,3584]{1,0:T(8,128)(2,1)} %convolution_convert_fusion), channel_id=1, source_target_pairs={{0,4},{4,0},{1,5},{5,1},{2,6},{6,2},{3,7},{7,3},{8,12},{12,8},{9,1... | collective-permute-start | bytes 11010056 | tf_op jit(solution)/shard_map/ppermute | solution.py:214
  169.8 26.5 %collective-permute-start.8 = (bf16[128,2048]{1,0:T(8,128)(2,1)S(1)}, bf16[128,2048]{1,0:T(8,128)(2,1)S(1)}, u32[]{:S(2)}, u32[]{:S(2)}) collective-permute-start(bf16[128,2048]{1,0:T(8,128)(2,1)S(1)} %get-tuple-element.26), channel_id=1, source_target_pairs={{0,3},{1,0},{2,1},{3,2},{4,7},{5,4},{6,5},{7,6},{8,11},{9,8},{10,9... | collective-permute-start | bytes 1572872 | tf_op jit(solution)/shard_map/ppermute | solution.py:214
  170.0 45.0 %collective-permute-start.7 = (bf16[128,2048]{1,0:T(8,128)(2,1)S(1)}, bf16[128,2048]{1,0:T(8,128)(2,1)S(1)}, u32[]{:S(2)}, u32[]{:S(2)}) collective-permute-start(bf16[128,2048]{1,0:T(8,128)(2,1)S(1)} %get-tuple-element.27), channel_id=1, source_target_pairs={{0,2},{1,3},{2,0},{3,1},{4,6},{5,7},{6,4},{7,5},{8,10},{9,11},{10,... | collective-permute-start | bytes 1572872 | tf_op jit(solution)/shard_map/ppermute | solution.py:214
  170.3 68.7 %collective-permute-start.6 = (bf16[128,2048]{1,0:T(8,128)(2,1)S(1)}, bf16[128,2048]{1,0:T(8,128)(2,1)S(1)}, u32[]{:S(2)}, u32[]{:S(2)}) collective-permute-start(bf16[128,2048]{1,0:T(8,128)(2,1)S(1)} %get-tuple-element.25), channel_id=1, source_target_pairs={{0,1},{1,2},{2,3},{3,0},{4,5},{5,6},{6,7},{7,4},{8,9},{9,10},{10,1... | collective-permute-start | bytes 1572872 | tf_op jit(solution)/shard_map/ppermute | solution.py:214
  180.6 12.4 %copy-start.5 = (bf16[512,3584]{1,0:T(8,128)(2,1)}, bf16[512,3584]{1,0:T(8,128)(2,1)S(1)}, u32[]{:S(2)}) copy-start(bf16[512,3584]{1,0:T(8,128)(2,1)S(1)} %multiply_convert_fusion.rhs_ref) | copy-start | bytes 11010052
  193.0 48.2 %copy-start.1 = (bf16[512,2048]{1,0:T(8,128)(2,1)S(1)}, bf16[512,2048]{1,0:T(8,128)(2,1)}, u32[]{:S(2)}) copy-start(bf16[512,2048]{1,0:T(8,128)(2,1)} %copy-done) | copy-start | bytes 6291460
  193.0 48.2 %copy-start.3 = (s32[1792]{0:T(1024)S(1)}, s32[1792]{0:T(1024)}, u32[]{:S(2)}) copy-start(s32[1792]{0:T(1024)} %fusion.2.slot_ref) | copy-start | bytes 21508
  194.2 96.8 %collective-permute-start.17 = (bf16[128,2048]{1,0:T(8,128)(2,1)}, bf16[128,2048]{1,0:T(8,128)(2,1)S(1)}, u32[]{:S(2)}, u32[]{:S(2)}) collective-permute-start(bf16[128,2048]{1,0:T(8,128)(2,1)} %get-tuple-element.23), channel_id=1, source_target_pairs={{0,3},{1,0},{2,1},{3,2},{4,7},{5,4},{6,5},{7,6},{8,11},{9,8},{10,9... | collective-permute-start | bytes 1572872 | tf_op jit(solution)/shard_map/ppermute | solution.py:214
  194.3 96.7 %collective-permute-start.16 = (bf16[128,2048]{1,0:T(8,128)(2,1)}, bf16[128,2048]{1,0:T(8,128)(2,1)S(1)}, u32[]{:S(2)}, u32[]{:S(2)}) collective-permute-start(bf16[128,2048]{1,0:T(8,128)(2,1)} %get-tuple-element.24), channel_id=1, source_target_pairs={{0,2},{1,3},{2,0},{3,1},{4,6},{5,7},{6,4},{7,5},{8,10},{9,11},{10,... | collective-permute-start | bytes 1572872 | tf_op jit(solution)/shard_map/ppermute | solution.py:214
  196.3 94.6 %collective-permute-start.15 = (bf16[128,2048]{1,0:T(8,128)(2,1)S(1)}, bf16[128,2048]{1,0:T(8,128)(2,1)S(1)}, u32[]{:S(2)}, u32[]{:S(2)}) collective-permute-start(bf16[128,2048]{1,0:T(8,128)(2,1)S(1)} %get-tuple-element.22), channel_id=1, source_target_pairs={{0,1},{1,2},{2,3},{3,0},{4,5},{5,6},{6,7},{7,4},{8,9},{9,10},{10,1... | collective-permute-start | bytes 1572872 | tf_op jit(solution)/shard_map/ppermute | solution.py:214
  241.2 24.7 %copy-start.2 = (s32[1792]{0:T(1024)S(1)}, s32[1792]{0:T(1024)}, u32[]{:S(2)}) copy-start(s32[1792]{0:T(1024)} %fusion.3.slot_ref) | copy-start | bytes 21508
where the time goes:
time: 293 us; the launch traced here: 292 us
  waiting for transfers between devices  95.9 us (33%)
  Pallas kernels  81.7 us (28%)
  matrix products  49.2 us (17%)
  starting transfers between devices  35.2 us (12%)
  other arithmetic  22.7 us (8%)
  local copies, waits for them, and re-layouts  6.64 us (2%)
    ppermute x18, waiting for transfers between devices, moved(): return lax.ppermute(value, axis, pairs)  95.9 us
    pallas_call x2, Pallas kernels, packed_grad(): pl.pallas_call(functools.partial(grad_kernel, group=group, groups=groups,...  49.7 us
    dot_general x4, matrix products, product(): lax.dot_general(left, right, (dims, ((), ())), preferred_element_type=jnp...  49.2 us
    ppermute x18, starting transfers between devices, moved(): return lax.ppermute(value, axis, pairs)  35.2 us
    pallas_call x2, Pallas kernels, unpack(): pl.pallas_call(functools.partial(unpack_kernel, cols=cols, capacity=capac...  32 us
    convert_element_type x1, other arithmetic, body(): pre_grad = (hidden_grad * slope_of(pre)).astype(jnp.bfloat16)  7.09 us
  transfers between devices with their start and end apart: 18, of which 9 were waited for; matrix products, arithmetic and copies ran while one was open for 12% of the time, Pallas kernels for 28%

commit v1 on v0

--- a/solution.py
+++ b/solution.py
@@ -88,7 +88,7 @@
             out_specs=pl.BlockSpec((group, 1, half, cols * BLK), lambda h, r, s: (r, h, 0, 0)),
             scratch_shapes=[
                 pltpu.VMEM((2, capacity, half * BLK), jnp.bfloat16),
-                pltpu.VMEM((half * pitch, LANES), jnp.float32),
+                pltpu.VMEM(((half + 1) * pitch, LANES), jnp.float32),
                 pltpu.SemaphoreType.DMA((2, 4)),
             ],
         ),
@@ -100,61 +100,54 @@
     return dense.reshape(rows * BLK, cols * BLK)
 
 
+def parted(rows):
+    to = lax.broadcasted_iota(jnp.int32, (rows, rows), 0)
+    half = BLK // 2
+    source = to // BLK * BLK + to % half * 2 + to % BLK // half
+    return (lax.broadcasted_iota(jnp.int32, (rows, rows), 1) == source).astype(jnp.bfloat16)
+
+
 def grad_kernel(slot_ref, count_ref, lhs_ref, rhs_ref, out_ref, turned_ref, even_ref, odd_ref, stage_ref, *,
                 group, groups, cols, capacity, width, pairs, chunks):
     pitch = capacity + PADROWS
     half = BLK // 2
     step = pl.program_id(0)
+    span = group * BLK
     keep = low_half(half)
-
-    def multiply(n, res_ref):
-        base = pl.multiple_of(n * (pairs * LANES), pairs * LANES)
-        value = jnp.dot(turned_ref[...], rhs_ref[:, pl.ds(base, pairs * LANES)], preferred_element_type=jnp.float32)
+    buffers = (even_ref, odd_ref)
+
+    def multiply(n):
+        res_ref = buffers[n % 2]
+        value = jnp.dot(turned_ref[...], rhs_ref[:, n * pairs * LANES:(n + 1) * pairs * LANES],
+                        preferred_element_type=jnp.float32)
         for q in range(pairs):
             res_ref[q] = value[:, q * LANES:(q + 1) * LANES]
 
-    def scatter(at, res_ref):
-        valid = at >= 0
-        at = jnp.maximum(at, 0)
-        block_row = at // chunks * group
-        block_col = at % chunks * (2 * pairs)
+    def scatter(n):
+        res_ref = buffers[n % 2]
         for r in range(group):
             for q in range(pairs):
-                even = res_ref[q, pl.ds(r * BLK, half, stride=2), :]
-                odd = res_ref[q, pl.ds(r * BLK + 1, half, stride=2), :]
+                even = res_ref[q, r * BLK:r * BLK + half, :]
+                odd = res_ref[q, r * BLK + half:(r + 1) * BLK, :]
                 first = jnp.where(keep, even, pltpu.roll(odd, BLK, 1))
                 second = jnp.where(keep, pltpu.roll(even, BLK, 1), odd)
-                where = (block_row + r) * cols + block_col + 2 * q
-                one = jnp.where(valid, slot_ref[where], capacity)
-                two = jnp.where(valid, slot_ref[where + 1], capacity)
-                stage_ref[pl.ds(one, half, stride=pitch), :] = first
-                stage_ref[pl.ds(two, half, stride=pitch), :] = second
+                at = (step * group + r) * cols + 2 * (n * pairs + q)
+                stage_ref[pl.ds(slot_ref[at], half, stride=pitch), :] = first
+                stage_ref[pl.ds(slot_ref[at + 1], half, stride=pitch), :] = second
 
     @pl.when(step < groups)
     def _():
-        turned_ref[...] = lhs_ref[...].T
-        if chunks % 2:
-            def one_chunk(n, carry):
-                multiply(n, even_ref)
-                scatter(step * chunks + n, even_ref)
-                return carry
-
-            lax.fori_loop(0, chunks, one_chunk, 0)
-        else:
-            def two_chunks(m, carry):
-                at = step * chunks + 2 * m
-                multiply(2 * m, even_ref)
-                scatter(at - 1, odd_ref)
-                multiply(2 * m + 1, odd_ref)
-                scatter(at, even_ref)
-                return carry
-
-            lax.fori_loop(0, chunks // 2, two_chunks, 0)
-
-    if chunks % 2 == 0:
-        @pl.when(step == groups)
-        def _():
-            scatter(groups * chunks - 1, odd_ref)
+        part = 2 * BLK if span % (2 * BLK) == 0 else BLK
+        order = parted(part)
+        for m in range(span // part):
+            turned_ref[m * part:(m + 1) * part, :] = lax.dot_general(
+                order, lhs_ref[:, m * part:(m + 1) * part], (((1,), (1,)), ((), ())),
+                preferred_element_type=jnp.float32).astype(jnp.bfloat16)
+        for n in range(chunks):
+            multiply(n)
+            if n:
+                scatter(n - 1)
+        scatter(chunks - 1)
 
     @pl.when(step >= groups)
     def _():
@@ -180,7 +173,7 @@
     half = BLK // 2
     group = max(g for g in range(1, 9) if rows % g == 0 and g * BLK % LANES == 0 or g == rows)
     groups = rows // group
-    pairs = 2 if cols % 4 == 0 else 1
+    pairs = max(p for p in (1, 2, 4) if cols % (2 * p) == 0)
     width = 1024
     span = group * BLK
     emits = BLK * BLK // width
@@ -200,7 +193,7 @@
                 pltpu.VMEM((span, tokens), jnp.bfloat16),
                 pltpu.VMEM((pairs, span, LANES), jnp.float32),
                 pltpu.VMEM((pairs, span, LANES), jnp.float32),
-                pltpu.VMEM((half * pitch, LANES), jnp.float32),
+                pltpu.VMEM(((half + 1) * pitch, LANES), jnp.float32),
             ],
         ),
         compiler_params=pltpu.CompilerParams(
@@ -284,13 +277,14 @@
     up_slots, up_count = slots_of(up_mask[0], capacity)
     down_slots, down_count = slots_of(down_mask[0], capacity)
     tok_in = shifted(act_handoff, "pipe", 1)
+    up = unpack(up_blocks[0, 0, 0], up_slots, rows, cols)
+    tok_in = after(tok_in, up)
     grad_in = shifted(after(grad_handoff, tok_in), "pipe", -1)[0]
     tok_in = tok_in[0]
-    up = unpack(up_blocks[0, 0, 0], after(up_slots, tok_in), rows, cols)
-    tokens = near_gather(tok_in, (up,))
-    down = unpack(down_blocks[0, 0, 0], after(down_slots, up), cols, rows)
+    down = unpack(down_blocks[0, 0, 0], after(down_slots, tok_in), cols, rows)
+    tokens = near_gather(tok_in, (down,))
     part = product(tokens, up, ((1,), (0,)))
-    grads = near_gather(after(grad_in, tokens), (part,))
+    grads = near_gather(after(grad_in, down), (part,))
     pre = wide_sum([part] + row_others(part))
     hidden = jax.nn.silu(pre).astype(jnp.bfloat16)
     branch_part = product(hidden, down, ((1,), (0,)))

time: 293 us -> 273 us (0.932)
  the two profiles are of different devices: /device:TPU:21 before, /device:TPU:18 now
where the time goes in v1:
time: 273 us; the launch traced here: 272 us
  waiting for transfers between devices  99.3 us (36%)
  Pallas kernels  68.2 us (25%)
  matrix products  44.8 us (16%)
  starting transfers between devices  35.1 us (13%)
  other arithmetic  17.7 us (6%)
  local copies, waits for them, and re-layouts  6.4 us (2%)
    ppermute x18, waiting for transfers between devices, moved(): return lax.ppermute(value, axis, pairs)  99.3 us
    dot_general x4, matrix products, product(): lax.dot_general(left, right, (dims, ((), ())), preferred_element_type=jnp...  44.8 us
    pallas_call x2, Pallas kernels, packed_grad(): pl.pallas_call(functools.partial(grad_kernel, group=group, groups=groups,...  36.2 us
    ppermute x18, starting transfers between devices, moved(): return lax.ppermute(value, axis, pairs)  35.1 us
    pallas_call x2, Pallas kernels, unpack(): pl.pallas_call(functools.partial(unpack_kernel, cols=cols, capacity=capac...  32 us
    convert_element_type x1, other arithmetic, body(): pre_grad = (hidden_grad * slope_of(pre)).astype(jnp.bfloat16)  7 us
  transfers between devices with their start and end apart: 18, of which 10 were waited for; matrix products, arithmetic and copies ran while one was open for 11% of the time, Pallas kernels for 25%

profile of v1, /device:TPU:18, one launch (start us, length us, event | category | flops | bytes accessed | tf_op | source)
XLA Modules:
  0.0 272.5 jit_solution(1623821437316351581)
XLA Ops:
  0.6 1.5 collective-permute-start
  2.2 0.8 reshape_squeeze.6
  3.0 0.8 reshape.44
  3.8 0.3 reduce-window.16
  4.1 0.1 slice.50
  4.2 0.1 slice_reduce_fusion.1
  4.3 0.7 fusion.3.slot_ref
  5.0 15.2 %unpack_tile.2 = bf16[32,2,32,3584]{3,2,1,0:T(8,128)(2,1)} custom-call(s32[1792]{0:T(1024)} %fusion.3.slot_ref, bf16[1024,4096]{1,0:T(8,128)(2,1)} %bitcast.37), custom_call_target="tpu_custom_call" | custom-call | tf_op jit(solution)/shard_map/unpack_tile/pallas_call | solution.py:81
  20.2 0.0 copy-start.7
  20.2 0.4 collective-permute-start.1
  20.6 0.1 copy.10
  20.7 0.1 reshape_squeeze.7
  20.8 0.1 reshape.47
  20.8 0.3 reduce-window.24
  21.1 0.1 slice.52
  21.2 0.1 slice_reduce_fusion
  21.3 0.7 fusion.2.slot_ref
  22.0 4.6 %collective-permute-start.3 = (bf16[128,2048]{1,0:T(8,128)(2,1)S(1)}, bf16[128,2048]{1,0:T(8,128)(2,1)S(1)}, u32[]{:S(2)}, u32[]{:S(2)}) collective-permute-start(bf16[128,2048]{1,0:T(8,128)(2,1)S(1)} %bitcast.42), channel_id=1, source_target_pairs={{1,0},{2,1},{3,2},{5,4},{6,5},{7,6},{9,8},{10,9},{11,10},{13,12},{... | collective-permute-start | bytes 1572872 | tf_op jit(solution)/shard_map/ppermute | solution.py:207
  26.6 1.9 collective-permute-start.4
  28.5 16.8 %unpack_tile.3 = bf16[56,2,32,2048]{3,2,1,0:T(8,128)(2,1)} custom-call(s32[1792]{0:T(1024)} %fusion.2.slot_ref, bf16[1024,4096]{1,0:T(8,128)(2,1)} %bitcast.38), custom_call_target="tpu_custom_call" | custom-call | tf_op jit(solution)/shard_map/unpack_tile/pallas_call | solution.py:81
  45.3 0.0 copy-start.11
  45.3 4.0 %collective-permute-start.2 = (bf16[128,2048]{1,0:T(8,128)(2,1)S(1)}, bf16[128,2048]{1,0:T(8,128)(2,1)S(1)}, u32[]{:S(2)}, u32[]{:S(2)}) collective-permute-start(bf16[128,2048]{1,0:T(8,128)(2,1)S(1)} %collective-permute-done.1), channel_id=1, source_target_pairs={{1,0},{2,3},{5,4},{6,7},{9,8},{10,11},{13,12},{14,15},{17,16},{18,... | collective-permute-start | bytes 1572872 | tf_op jit(solution)/shard_map/ppermute | solution.py:207
  49.4 4.7 %collective-permute-done.3 = bf16[128,2048]{1,0:T(8,128)(2,1)S(1)} collective-permute-done((bf16[128,2048]{1,0:T(8,128)(2,1)S(1)}, bf16[128,2048]{1,0:T(8,128)(2,1)S(1)}, u32[]{:S(2)}, u32[]{:S(2)}) %collective-permute-start.3) | collective-permute-done | bytes 524320 | tf_op jit(solution)/shard_map/ppermute | solution.py:207
  54.0 3.1 %collective-permute-done.4 = bf16[128,2048]{1,0:T(8,128)(2,1)S(1)} collective-permute-done((bf16[128,2048]{1,0:T(8,128)(2,1)S(1)}, bf16[128,2048]{1,0:T(8,128)(2,1)S(1)}, u32[]{:S(2)}, u32[]{:S(2)}) %collective-permute-start.4) | collective-permute-done | bytes 524320 | tf_op jit(solution)/shard_map/ppermute | solution.py:207
  57.1 4.4 %collective-permute-done.2 = bf16[128,2048]{1,0:T(8,128)(2,1)S(1)} collective-permute-done((bf16[128,2048]{1,0:T(8,128)(2,1)S(1)}, bf16[128,2048]{1,0:T(8,128)(2,1)S(1)}, u32[]{:S(2)}, u32[]{:S(2)}) %collective-permute-start.2) | collective-permute-done | bytes 524320 | tf_op jit(solution)/shard_map/ppermute | solution.py:207
  61.5 0.1 broadcast_select_fusion.3
  61.6 0.0 copy-start.14
  61.7 11.3 %convolution_convert_fusion.1 = bf16[512,3584]{1,0:T(8,128)(2,1)S(1)} fusion(bf16[2048,3584]{1,0:T(8,128)(2,1)} %bitcast.31, bf16[128,2048]{1,0:T(8,128)(2,1)S(1)} %get-tuple-element.31, bf16[128,2048]{1,0:T(8,128)(2,1)} %copy-done.11, bf16[128,2048]{1,0:T(8,128)(2,1)S(1)} %get-tuple-element.30, bf16[128,2048]{1,0:T(8,128)(2,1)S(1)} %bitcast.44), kind=kOutput, calls=%fused_computation.5 | convolution fusion | flops 7526416384 | bytes 20447232 | tf_op jit(solution)/shard_map/dot_general | solution.py:238
  73.0 0.1 collective-permute-start.5
  73.1 0.6 collective-permute-start.9
  73.6 14.6 %collective-permute-done.9 = bf16[1,128,2048]{2,1,0:T(8,128)(2,1)S(1)} collective-permute-done((bf16[1,128,2048]{2,1,0:T(8,128)(2,1)S(1)}, bf16[1,128,2048]{2,1,0:T(8,128)(2,1)S(1)}, u32[]{:S(2)}, u32[]{:S(2)}) %collective-permute-start.9) | collective-permute-done | bytes 524320 | tf_op jit(solution)/shard_map/ppermute | solution.py:207
  88.3 0.2 collective-permute-start.10
  88.5 5.6 %collective-permute-start.12 = (bf16[128,2048]{1,0:T(8,128)(2,1)S(1)}, bf16[128,2048]{1,0:T(8,128)(2,1)S(1)}, u32[]{:S(2)}, u32[]{:S(2)}) collective-permute-start(bf16[128,2048]{1,0:T(8,128)(2,1)S(1)} %bitcast.47), channel_id=1, source_target_pairs={{1,0},{2,1},{3,2},{5,4},{6,5},{7,6},{9,8},{10,9},{11,10},{13,12},{... | collective-permute-start | bytes 1572872 | tf_op jit(solution)/shard_map/ppermute | solution.py:207
  94.1 1.9 collective-permute-start.13
  96.1 16.0 %collective-permute-done.10 = bf16[128,2048]{1,0:T(8,128)(2,1)S(1)} collective-permute-done((bf16[128,2048]{1,0:T(8,128)(2,1)S(1)}, bf16[128,2048]{1,0:T(8,128)(2,1)S(1)}, u32[]{:S(2)}, u32[]{:S(2)}) %collective-permute-start.10) | collective-permute-done | bytes 524320 | tf_op jit(solution)/shard_map/ppermute | solution.py:207
  112.1 5.5 %collective-permute-start.11 = (bf16[128,2048]{1,0:T(8,128)(2,1)S(1)}, bf16[128,2048]{1,0:T(8,128)(2,1)S(1)}, u32[]{:S(2)}, u32[]{:S(2)}) collective-permute-start(bf16[128,2048]{1,0:T(8,128)(2,1)S(1)} %collective-permute-done.10), channel_id=1, source_target_pairs={{1,0},{2,3},{5,4},{6,7},{9,8},{10,11},{13,12},{14,15},{17,16},{18,... | collective-permute-start | bytes 1572872 | tf_op jit(solution)/shard_map/ppermute | solution.py:207
  117.5 4.5 %collective-permute-done.12 = bf16[128,2048]{1,0:T(8,128)(2,1)S(1)} collective-permute-done((bf16[128,2048]{1,0:T(8,128)(2,1)S(1)}, bf16[128,2048]{1,0:T(8,128)(2,1)S(1)}, u32[]{:S(2)}, u32[]{:S(2)}) %collective-permute-start.12) | collective-permute-done | bytes 524320 | tf_op jit(solution)/shard_map/ppermute | solution.py:207
  122.0 3.1 %collective-permute-done.13 = bf16[128,2048]{1,0:T(8,128)(2,1)S(1)} collective-permute-done((bf16[128,2048]{1,0:T(8,128)(2,1)S(1)}, bf16[128,2048]{1,0:T(8,128)(2,1)S(1)}, u32[]{:S(2)}, u32[]{:S(2)}) %collective-permute-start.13) | collective-permute-done | bytes 524320 | tf_op jit(solution)/shard_map/ppermute | solution.py:207
  125.1 3.9 %collective-permute-done.11 = bf16[128,2048]{1,0:T(8,128)(2,1)S(1)} collective-permute-done((bf16[128,2048]{1,0:T(8,128)(2,1)S(1)}, bf16[128,2048]{1,0:T(8,128)(2,1)S(1)}, u32[]{:S(2)}, u32[]{:S(2)}) %collective-permute-start.11) | collective-permute-done | bytes 524320 | tf_op jit(solution)/shard_map/ppermute | solution.py:207
  129.1 0.1 broadcast_select_fusion.2
  129.1 0.1 pad_maximum_fusion.1.rhs_ref
  129.3 0.0 copy-start.4
  129.3 2.1 multiply_convert_fusion.1.lhs_ref
  131.4 1.8 copy-done.6
  133.2 9.0 %convolution_convert_fusion.3 = bf16[512,2048]{1,0:T(8,128)(2,1)} fusion(bf16[512,3584]{1,0:T(8,128)(2,1)S(1)} %multiply_convert_fusion.1.lhs_ref, bf16[3584,2048]{1,0:T(8,128)(2,1)S(1)} %bitcast.36), kind=kOutput, calls=%fused_computation.7 | convolution fusion | flops 7517241344 | bytes 20447232 | tf_op jit(solution)/shard_map/dot_general | solution.py:238
  142.2 12.3 %convolution_convert_fusion = bf16[512,3584]{1,0:T(8,128)(2,1)} fusion(bf16[512,2048]{1,0:T(8,128)(2,1)S(1)} %pad_maximum_fusion.1.rhs_ref, bf16[3584,2048]{1,0:T(8,128)(2,1)} %bitcast.33), kind=kOutput, calls=%fused_computation.4 | convolution fusion | flops 7518027776 | bytes 20447232 | tf_op jit(solution)/shard_map/dot_general | solution.py:238
  154.5 0.7 reduce_sum.18
  155.2 0.7 reduce_sum.19
  155.9 1.5 pad_maximum_fusion.lhs_ref
  157.4 2.2 fusion.5
  159.6 0.1 collective-permute-start.8
  159.7 4.8 %collective-permute-start.7 = (bf16[128,2048]{1,0:T(8,128)(2,1)S(1)}, bf16[128,2048]{1,0:T(8,128)(2,1)S(1)}, u32[]{:S(2)}, u32[]{:S(2)}) collective-permute-start(bf16[128,2048]{1,0:T(8,128)(2,1)S(1)} %get-tuple-element.27), channel_id=1, source_target_pairs={{0,2},{1,3},{2,0},{3,1},{4,6},{5,7},{6,4},{7,5},{8,10},{9,11},{10,... | collective-permute-start | bytes 1572872 | tf_op jit(solution)/shard_map/ppermute | solution.py:207
  164.5 0.0 collective-permute-start.6
  164.6 7.0 %multiply_convert_fusion.rhs_ref = bf16[512,3584]{1,0:T(8,128)(2,1)} fusion(bf16[512,3584]{1,0:T(8,128)(2,1)} %collective-permute-done.14, bf16[512,3584]{1,0:T(8,128)(2,1)} %convolution_convert_fusion, bf16[512,3584]{1,0:T(8,128)(2,1)S(1)} %copy-done.5, bf16[512,3584]{1,0:T(8,128)(2,1)S(1)} %copy-done.3), kind=kLoop, calls=%fused_computation | loop fusion | flops 27525120 | bytes 18350080 | tf_op jit(solution)/shard_map/convert_element_type | solution.py:294
  171.6 12.2 %convolution_convert_fusion.2 = bf16[512,2048]{1,0:T(8,128)(2,1)S(1)} fusion(bf16[512,3584]{1,0:T(8,128)(2,1)} %multiply_convert_fusion.rhs_ref, bf16[2048,3584]{1,0:T(8,128)(2,1)} %bitcast.32), kind=kOutput, calls=%fused_computation.6 | convolution fusion | flops 7517241344 | bytes 20447232 | tf_op jit(solution)/shard_map/dot_general | solution.py:238
  183.8 0.1 fusion.4
  183.9 2.1 collective-permute-start.17
  186.0 1.8 collective-permute-start.16
  187.8 18.0 %collective-permute-done.7 = bf16[128,2048]{1,0:T(8,128)(2,1)S(1)} collective-permute-done((bf16[128,2048]{1,0:T(8,128)(2,1)S(1)}, bf16[128,2048]{1,0:T(8,128)(2,1)S(1)}, u32[]{:S(2)}, u32[]{:S(2)}) %collective-permute-start.7) | collective-permute-done | bytes 524320 | tf_op jit(solution)/shard_map/ppermute | solution.py:207
  205.8 27.0 %collective-permute-done.6 = bf16[128,2048]{1,0:T(8,128)(2,1)S(1)} collective-permute-done((bf16[128,2048]{1,0:T(8,128)(2,1)S(1)}, bf16[128,2048]{1,0:T(8,128)(2,1)S(1)}, u32[]{:S(2)}, u32[]{:S(2)}) %collective-permute-start.6) | collective-permute-done | bytes 524320 | tf_op jit(solution)/shard_map/ppermute | solution.py:207
  232.8 2.3 fusion
  235.0 18.2 %packed_grad.2 = bf16[1024,4096]{1,0:T(8,128)(2,1)} custom-call(s32[1792]{0:T(1024)S(1)} %copy-done.1, s32[1]{0:T(128)} %bitcast.11.count_ref, bf16[512,3584]{1,0:T(8,128)(2,1)} %copy-done.6, bf16[512,2048]{1,0:T(8,128)(2,1)S(1)} %pad_maximum_fusion.1.rhs_ref), custom_call_target="tpu_custom_call" | custom-call | tf_op jit(solution)/shard_map/packed_grad/pallas_call | solution.py:180
  253.2 18.0 %packed_grad.3 = bf16[1024,4096]{1,0:T(8,128)(2,1)} custom-call(s32[1792]{0:T(1024)S(1)} %copy-done, s32[1]{0:T(128)} %bitcast.10.count_ref, bf16[512,2048]{1,0:T(8,128)(2,1)S(1)} %pad_maximum_fusion.lhs_ref, bf16[512,3584]{1,0:T(8,128)(2,1)} %multiply_convert_fusion.rhs_ref), custom_call_target="tpu_custom_call" | custom-call | tf_op jit(solution)/shard_map/packed_grad/pallas_call | solution.py:180
  271.3 1.2 fusion.1
  (46 shorter events, 0.2 us)
Async XLA Ops:
  0.6 19.6 %collective-permute-start = (bf16[1,128,2048]{2,1,0:T(8,128)(2,1)}, bf16[1,128,2048]{2,1,0:T(8,128)(2,1)S(1)}, u32[]{:S(2)}, u32[]{:S(2)}) collective-permute-start(bf16[1,128,2048]{2,1,0:T(8,128)(2,1)} %param.6), channel_id=1, source_target_pairs={{0,8},{8,16},{16,24},{24,0},{1,9},{9,17},{17,25},{25,1},{2,10},{10... | collective-permute-start | bytes 1572872 | tf_op jit(solution)/shard_map/ppermute | solution.py:207
  5.0 15.6 %copy-start.13 = (s32[1,56,32]{1,2,0:T(8,128)S(1)}, s32[1,56,32]{1,2,0:T(8,128)}, u32[]{:S(2)}) copy-start(s32[1,56,32]{1,2,0:T(8,128)} %param.11) | copy-start | bytes 21508
  20.2 41.4 %copy-start.7 = (bf16[1,128,2048]{2,1,0:T(8,128)(2,1)}, bf16[1,128,2048]{2,1,0:T(8,128)(2,1)S(1)}, u32[]{:S(2)}) copy-start(bf16[1,128,2048]{2,1,0:T(8,128)(2,1)S(1)} %collective-permute-done) | copy-start | bytes 1572868
  20.2 25.1 %collective-permute-start.1 = (bf16[128,2048]{1,0:T(8,128)(2,1)S(1)}, bf16[128,2048]{1,0:T(8,128)(2,1)S(1)}, u32[]{:S(2)}, u32[]{:S(2)}) collective-permute-start(bf16[128,2048]{1,0:T(8,128)(2,1)S(1)} %bitcast.41), channel_id=1, source_target_pairs={{0,2},{1,3},{2,0},{3,1},{4,6},{5,7},{6,4},{7,5},{8,10},{9,11},{10,... | collective-permute-start | bytes 1572872 | tf_op jit(solution)/shard_map/ppermute | solution.py:207
  22.0 32.0 %collective-permute-start.3 = (bf16[128,2048]{1,0:T(8,128)(2,1)S(1)}, bf16[128,2048]{1,0:T(8,128)(2,1)S(1)}, u32[]{:S(2)}, u32[]{:S(2)}) collective-permute-start(bf16[128,2048]{1,0:T(8,128)(2,1)S(1)} %bitcast.42), channel_id=1, source_target_pairs={{1,0},{2,1},{3,2},{5,4},{6,5},{7,6},{9,8},{10,9},{11,10},{13,12},{... | collective-permute-start | bytes 1572872 | tf_op jit(solution)/shard_map/ppermute | solution.py:207
  26.6 30.5 %collective-permute-start.4 = (bf16[128,2048]{1,0:T(8,128)(2,1)S(1)}, bf16[128,2048]{1,0:T(8,128)(2,1)S(1)}, u32[]{:S(2)}, u32[]{:S(2)}) collective-permute-start(bf16[128,2048]{1,0:T(8,128)(2,1)S(1)} %bitcast.43), channel_id=1, source_target_pairs={{0,1},{1,2},{2,3},{4,5},{5,6},{6,7},{8,9},{9,10},{10,11},{12,13},{... | collective-permute-start | bytes 1572872 | tf_op jit(solution)/shard_map/ppermute | solution.py:207
  45.3 11.8 %copy-start.11 = (bf16[128,2048]{1,0:T(8,128)(2,1)}, bf16[128,2048]{1,0:T(8,128)(2,1)S(1)}, u32[]{:S(2)}) copy-start(bf16[128,2048]{1,0:T(8,128)(2,1)S(1)} %collective-permute-done.1) | copy-start | bytes 1572868
  45.3 16.2 %collective-permute-start.2 = (bf16[128,2048]{1,0:T(8,128)(2,1)S(1)}, bf16[128,2048]{1,0:T(8,128)(2,1)S(1)}, u32[]{:S(2)}, u32[]{:S(2)}) collective-permute-start(bf16[128,2048]{1,0:T(8,128)(2,1)S(1)} %collective-permute-done.1), channel_id=1, source_target_pairs={{1,0},{2,3},{5,4},{6,7},{9,8},{10,11},{13,12},{14,15},{17,16},{18,... | collective-permute-start | bytes 1572872 | tf_op jit(solution)/shard_map/ppermute | solution.py:207
  61.5 71.7 %slice-start = ((s8[14680064]{0:T(1024)(128)(4,1)}), s8[4194304]{0:T(1024)(128)(4,1)S(1)}, s32[]{:S(2)}) async-start(s8[14680064]{0:T(1024)(128)(4,1)} %bitcast.34), calls=%async_computation | async-start | bytes 8388608
  61.6 11.4 %copy-start.14 = (bf16[1,128,2048]{2,1,0:T(8,128)(2,1)S(1)}, bf16[1,128,2048]{2,1,0:T(8,128)(2,1)}, u32[]{:S(2)}) copy-start(bf16[1,128,2048]{2,1,0:T(8,128)(2,1)} %param.7) | copy-start | bytes 1572868
  61.6 71.6 %slice-start.1 = ((s8[14680064]{0:T(1024)(128)(4,1)}), s8[4194304]{0:T(1024)(128)(4,1)S(1)}, s32[]{:S(2)}) async-start(s8[14680064]{0:T(1024)(128)(4,1)} %bitcast.34), calls=%async_computation.1 | async-start | bytes 8388608
  61.6 71.6 %slice-start.2 = ((s8[14680064]{0:T(1024)(128)(4,1)}), s8[4194304]{0:T(1024)(128)(4,1)S(1)}, s32[]{:S(2)}) async-start(s8[14680064]{0:T(1024)(128)(4,1)} %bitcast.34), calls=%async_computation.2 | async-start | bytes 8388608
  61.7 71.6 %slice-start.3 = ((s8[14680064]{0:T(1024)(128)(4,1)}), s8[2097152]{0:T(1024)(128)(4,1)S(1)}, s32[]{:S(2)}) async-start(s8[14680064]{0:T(1024)(128)(4,1)} %bitcast.34), calls=%async_computation.3 | async-start | bytes 4194304
  73.0 58.5 %copy-start.2 = (bf16[512,3584]{1,0:T(8,128)(2,1)}, bf16[512,3584]{1,0:T(8,128)(2,1)S(1)}, u32[]{:S(2)}) copy-start(bf16[512,3584]{1,0:T(8,128)(2,1)S(1)} %convolution_convert_fusion.1) | copy-start | bytes 11010052
  73.0 56.3 %collective-permute-start.5 = (bf16[512,3584]{1,0:T(8,128)(2,1)S(1)}, bf16[512,3584]{1,0:T(8,128)(2,1)S(1)}, u32[]{:S(2)}, u32[]{:S(2)}) collective-permute-start(bf16[512,3584]{1,0:T(8,128)(2,1)S(1)} %convolution_convert_fusion.1), channel_id=1, source_target_pairs={{0,4},{4,0},{1,5},{5,1},{2,6},{6,2},{3,7},{7,3},{8,12},{12,8},{9,1... | collective-permute-start | bytes 11010056 | tf_op jit(solution)/shard_map/ppermute | solution.py:207
  73.1 15.2 %collective-permute-start.9 = (bf16[1,128,2048]{2,1,0:T(8,128)(2,1)S(1)}, bf16[1,128,2048]{2,1,0:T(8,128)(2,1)S(1)}, u32[]{:S(2)}, u32[]{:S(2)}) collective-permute-start(bf16[1,128,2048]{2,1,0:T(8,128)(2,1)S(1)} %copy-done.14), channel_id=1, source_target_pairs={{0,24},{8,0},{16,8},{24,16},{1,25},{9,1},{17,9},{25,17},{2,26},{10... | collective-permute-start | bytes 1572872 | tf_op jit(solution)/shard_map/ppermute | solution.py:207
  88.3 41.0 %copy-start.9 = (bf16[1,128,2048]{2,1,0:T(8,128)(2,1)}, bf16[1,128,2048]{2,1,0:T(8,128)(2,1)S(1)}, u32[]{:S(2)}) copy-start(bf16[1,128,2048]{2,1,0:T(8,128)(2,1)S(1)} %collective-permute-done.9) | copy-start | bytes 1572868
  88.3 23.8 %collective-permute-start.10 = (bf16[128,2048]{1,0:T(8,128)(2,1)S(1)}, bf16[128,2048]{1,0:T(8,128)(2,1)S(1)}, u32[]{:S(2)}, u32[]{:S(2)}) collective-permute-start(bf16[128,2048]{1,0:T(8,128)(2,1)S(1)} %bitcast.46), channel_id=1, source_target_pairs={{0,2},{1,3},{2,0},{3,1},{4,6},{5,7},{6,4},{7,5},{8,10},{9,11},{10,... | collective-permute-start | bytes 1572872 | tf_op jit(solution)/shard_map/ppermute | solution.py:207
  88.5 33.5 %collective-permute-start.12 = (bf16[128,2048]{1,0:T(8,128)(2,1)S(1)}, bf16[128,2048]{1,0:T(8,128)(2,1)S(1)}, u32[]{:S(2)}, u32[]{:S(2)}) collective-permute-start(bf16[128,2048]{1,0:T(8,128)(2,1)S(1)} %bitcast.47), channel_id=1, source_target_pairs={{1,0},{2,1},{3,2},{5,4},{6,5},{7,6},{9,8},{10,9},{11,10},{13,12},{... | collective-permute-start | bytes 1572872 | tf_op jit(solution)/shard_map/ppermute | solution.py:207
  94.1 31.0 %collective-permute-start.13 = (bf16[128,2048]{1,0:T(8,128)(2,1)S(1)}, bf16[128,2048]{1,0:T(8,128)(2,1)S(1)}, u32[]{:S(2)}, u32[]{:S(2)}) collective-permute-start(bf16[128,2048]{1,0:T(8,128)(2,1)S(1)} %bitcast.48), channel_id=1, source_target_pairs={{0,1},{1,2},{2,3},{4,5},{5,6},{6,7},{8,9},{9,10},{10,11},{12,13},{... | collective-permute-start | bytes 1572872 | tf_op jit(solution)/shard_map/ppermute | solution.py:207
  112.1 17.0 %collective-permute-start.11 = (bf16[128,2048]{1,0:T(8,128)(2,1)S(1)}, bf16[128,2048]{1,0:T(8,128)(2,1)S(1)}, u32[]{:S(2)}, u32[]{:S(2)}) collective-permute-start(bf16[128,2048]{1,0:T(8,128)(2,1)S(1)} %collective-permute-done.10), channel_id=1, source_target_pairs={{1,0},{2,3},{5,4},{6,7},{9,8},{10,11},{13,12},{14,15},{17,16},{18,... | collective-permute-start | bytes 1572872 | tf_op jit(solution)/shard_map/ppermute | solution.py:207
  129.3 2.1 copy-start.4
  131.4 1.8 copy-start.6
  142.2 12.3 %copy-start.12 = (s32[1,32,56]{2,1,0:T(8,128)S(1)}, s32[1,32,56]{2,1,0:T(8,128)}, u32[]{:S(2)}) copy-start(s32[1,32,56]{2,1,0:T(8,128)} %param.10) | copy-start | bytes 21508
  154.5 10.0 %collective-permute-start.14 = (bf16[512,3584]{1,0:T(8,128)(2,1)}, bf16[512,3584]{1,0:T(8,128)(2,1)}, u32[]{:S(2)}, u32[]{:S(2)}) collective-permute-start(bf16[512,3584]{1,0:T(8,128)(2,1)} %convolution_convert_fusion), channel_id=1, source_target_pairs={{0,4},{4,0},{1,5},{5,1},{2,6},{6,2},{3,7},{7,3},{8,12},{12,8},{9,1... | collective-permute-start | bytes 11010056 | tf_op jit(solution)/shard_map/ppermute | solution.py:207
  155.9 8.7 %copy-start.3 = (bf16[512,3584]{1,0:T(8,128)(2,1)S(1)}, bf16[512,3584]{1,0:T(8,128)(2,1)}, u32[]{:S(2)}) copy-start(bf16[512,3584]{1,0:T(8,128)(2,1)} %copy-done.2) | copy-start | bytes 11010052
  155.9 8.7 %copy-start.5 = (bf16[512,3584]{1,0:T(8,128)(2,1)S(1)}, bf16[512,3584]{1,0:T(8,128)(2,1)}, u32[]{:S(2)}) copy-start(bf16[512,3584]{1,0:T(8,128)(2,1)} %copy-done.4) | copy-start | bytes 11010052
  159.6 28.2 %collective-permute-start.8 = (bf16[128,2048]{1,0:T(8,128)(2,1)S(1)}, bf16[128,2048]{1,0:T(8,128)(2,1)S(1)}, u32[]{:S(2)}, u32[]{:S(2)}) collective-permute-start(bf16[128,2048]{1,0:T(8,128)(2,1)S(1)} %get-tuple-element.26), channel_id=1, source_target_pairs={{0,3},{1,0},{2,1},{3,2},{4,7},{5,4},{6,5},{7,6},{8,11},{9,8},{10,9... | collective-permute-start | bytes 1572872 | tf_op jit(solution)/shard_map/ppermute | solution.py:207
  159.7 46.1 %collective-permute-start.7 = (bf16[128,2048]{1,0:T(8,128)(2,1)S(1)}, bf16[128,2048]{1,0:T(8,128)(2,1)S(1)}, u32[]{:S(2)}, u32[]{:S(2)}) collective-permute-start(bf16[128,2048]{1,0:T(8,128)(2,1)S(1)} %get-tuple-element.27), channel_id=1, source_target_pairs={{0,2},{1,3},{2,0},{3,1},{4,6},{5,7},{6,4},{7,5},{8,10},{9,11},{10,... | collective-permute-start | bytes 1572872 | tf_op jit(solution)/shard_map/ppermute | solution.py:207
  164.5 68.2 %collective-permute-start.6 = (bf16[128,2048]{1,0:T(8,128)(2,1)S(1)}, bf16[128,2048]{1,0:T(8,128)(2,1)S(1)}, u32[]{:S(2)}, u32[]{:S(2)}) collective-permute-start(bf16[128,2048]{1,0:T(8,128)(2,1)S(1)} %get-tuple-element.25), channel_id=1, source_target_pairs={{0,1},{1,2},{2,3},{3,0},{4,5},{5,6},{6,7},{7,4},{8,9},{9,10},{10,1... | collective-permute-start | bytes 1572872 | tf_op jit(solution)/shard_map/ppermute | solution.py:207
  171.6 61.2 %copy-start.8 = (bf16[1,128,2048]{2,1,0:T(8,128)(2,1)S(1)}, bf16[1,128,2048]{2,1,0:T(8,128)(2,1)}, u32[]{:S(2)}) copy-start(bf16[1,128,2048]{2,1,0:T(8,128)(2,1)} %copy-done.7) | copy-start | bytes 1572868
  183.7 51.3 %copy-start.1 = (s32[1792]{0:T(1024)S(1)}, s32[1792]{0:T(1024)}, u32[]{:S(2)}) copy-start(s32[1792]{0:T(1024)} %fusion.2.slot_ref) | copy-start | bytes 21508
  183.9 87.3 %collective-permute-start.17 = (bf16[128,2048]{1,0:T(8,128)(2,1)S(1)}, bf16[128,2048]{1,0:T(8,128)(2,1)S(1)}, u32[]{:S(2)}, u32[]{:S(2)}) collective-permute-start(bf16[128,2048]{1,0:T(8,128)(2,1)S(1)} %get-tuple-element.23), channel_id=1, source_target_pairs={{0,3},{1,0},{2,1},{3,2},{4,7},{5,4},{6,5},{7,6},{8,11},{9,8},{10,9... | collective-permute-start | bytes 1572872 | tf_op jit(solution)/shard_map/ppermute | solution.py:207
  186.0 85.3 %collective-permute-start.16 = (bf16[128,2048]{1,0:T(8,128)(2,1)S(1)}, bf16[128,2048]{1,0:T(8,128)(2,1)S(1)}, u32[]{:S(2)}, u32[]{:S(2)}) collective-permute-start(bf16[128,2048]{1,0:T(8,128)(2,1)S(1)} %get-tuple-element.24), channel_id=1, source_target_pairs={{0,2},{1,3},{2,0},{3,1},{4,6},{5,7},{6,4},{7,5},{8,10},{9,11},{10,... | collective-permute-start | bytes 1572872 | tf_op jit(solution)/shard_map/ppermute | solution.py:207
  187.8 83.5 %collective-permute-start.15 = (bf16[128,2048]{1,0:T(8,128)(2,1)S(1)}, bf16[128,2048]{1,0:T(8,128)(2,1)S(1)}, u32[]{:S(2)}, u32[]{:S(2)}) collective-permute-start(bf16[128,2048]{1,0:T(8,128)(2,1)S(1)} %get-tuple-element.22), channel_id=1, source_target_pairs={{0,1},{1,2},{2,3},{3,0},{4,5},{5,6},{6,7},{7,4},{8,9},{9,10},{10,1... | collective-permute-start | bytes 1572872 | tf_op jit(solution)/shard_map/ppermute | solution.py:207
  235.0 18.2 %copy-start = (s32[1792]{0:T(1024)S(1)}, s32[1792]{0:T(1024)}, u32[]{:S(2)}) copy-start(s32[1792]{0:T(1024)} %fusion.3.slot_ref) | copy-start | bytes 21508
  253.2 18.1 %copy-start.10 = (bf16[1,128,2048]{2,1,0:T(8,128)(2,1)S(1)}, bf16[1,128,2048]{2,1,0:T(8,128)(2,1)}, u32[]{:S(2)}) copy-start(bf16[1,128,2048]{2,1,0:T(8,128)(2,1)} %copy-done.9) | copy-start | bytes 1572868

commit v2 on v1

--- a/solution.py
+++ b/solution.py
@@ -77,7 +77,7 @@
     capacity = packed.shape[0]
     pitch = capacity + PADROWS
     half = BLK // 2
-    group = largest_part(rows, 8)
+    group = largest_part(rows, 16)
     dense = pl.pallas_call(
         functools.partial(unpack_kernel, cols=cols, capacity=capacity, group=group),
         out_shape=jax.ShapeDtypeStruct((rows, 2, half, cols * BLK), jnp.bfloat16),
@@ -98,6 +98,82 @@
         name="unpack_tile",
     )(slots, packed)
     return dense.reshape(rows * BLK, cols * BLK)
+
+
+def unpack_half_kernel(slot_ref, packed_ref, *refs, cols, capacity, group, part):
+    out_ref, raw_ref, stage_ref, sems = refs[-4:]
+    pitch = capacity + PADROWS
+    half = BLK // 2
+    step = pl.program_id(0)
+    pieces = sems.shape[0]
+    piece = capacity // pieces
+
+    @pl.when(step == 0)
+    def _():
+        chunk = 32
+        copies = [
+            pltpu.make_async_copy(
+                packed_ref.at[pl.ds(p * piece, piece), pl.ds(part * half * BLK, half * BLK)],
+                raw_ref.at[pl.ds(p * piece, piece), :], sems.at[p])
+            for p in range(pieces)
+        ]
+        for copy in copies:
+            copy.start()
+        for i in range(half):
+            stage_ref[pl.ds(i * pitch + capacity, 8), :] = jnp.zeros((8, LANES), jnp.float32)
+
+        keep = low_half(chunk)
+
+        def stage(at, carry):
+            base = pl.multiple_of(at * chunk, chunk)
+            for tile in range(half // 2):
+                value = raw_ref[pl.ds(base, chunk), tile * LANES:(tile + 1) * LANES].astype(jnp.float32)
+                swapped = pltpu.roll(value, BLK, 1)
+                stage_ref[pl.ds(2 * tile * pitch + base, chunk), :] = jnp.where(keep, value, swapped)
+                stage_ref[pl.ds((2 * tile + 1) * pitch + base, chunk), :] = jnp.where(keep, swapped, value)
+            return carry
+
+        for p, copy in enumerate(copies):
+            copy.wait()
+            lax.fori_loop(p * piece // chunk, (p + 1) * piece // chunk, stage, 0)
+
+    keep = low_half(half)
+
+    def block_row(r, carry):
+        at = (step * group + r) * cols
+        for pair in range(cols // 2):
+            left = stage_ref[pl.ds(slot_ref[at + 2 * pair], half, stride=pitch), :]
+            right = stage_ref[pl.ds(slot_ref[at + 2 * pair + 1], half, stride=pitch), :]
+            out_ref[r, 0, :, pair * LANES:(pair + 1) * LANES] = jnp.where(keep, left, right).astype(jnp.bfloat16)
+        return carry
+
+    lax.fori_loop(0, group, block_row, 0)
+
+
+def unpack_half(packed, slots, rows, cols, part, previous=None):
+    capacity = packed.shape[0]
+    half = BLK // 2
+    group = largest_part(rows, 16)
+    anywhere = pl.BlockSpec(memory_space=pl.ANY)
+    given = () if previous is None else (previous,)
+    return pl.pallas_call(
+        functools.partial(unpack_half_kernel, cols=cols, capacity=capacity, group=group, part=part),
+        out_shape=jax.ShapeDtypeStruct((rows, 2, half, cols * BLK), jnp.bfloat16),
+        grid_spec=pltpu.PrefetchScalarGridSpec(
+            num_scalar_prefetch=1,
+            grid=(rows // group,),
+            in_specs=[anywhere] * (1 + len(given)),
+            out_specs=pl.BlockSpec((group, 1, half, cols * BLK), lambda r, s: (r, part, 0, 0)),
+            scratch_shapes=[
+                pltpu.VMEM((capacity, half * BLK), jnp.bfloat16),
+                pltpu.VMEM(((half + 1) * (capacity + PADROWS), LANES), jnp.float32),
+                pltpu.SemaphoreType.DMA((4,)),
+            ],
+        ),
+        input_output_aliases={2: 0} if given else {},
+        compiler_params=pltpu.CompilerParams(dimension_semantics=("arbitrary",), vmem_limit_bytes=60 << 20),
+        name="unpack_half",
+    )(slots, packed, *given)
 
 
 def parted(rows):
@@ -281,8 +357,10 @@
     tok_in = after(tok_in, up)
     grad_in = shifted(after(grad_handoff, tok_in), "pipe", -1)[0]
     tok_in = tok_in[0]
-    down = unpack(down_blocks[0, 0, 0], after(down_slots, tok_in), cols, rows)
+    down = unpack_half(down_blocks[0, 0, 0], after(down_slots, tok_in), cols, rows, 0)
     tokens = near_gather(tok_in, (down,))
+    down = unpack_half(down_blocks[0, 0, 0], down_slots, cols, rows, 1, down)
+    down = down.reshape(cols * BLK, rows * BLK)
     part = product(tokens, up, ((1,), (0,)))
     grads = near_gather(after(grad_in, down), (part,))
     pre = wide_sum([part] + row_others(part))

time: 273 us -> 273 us (level)
  the two profiles are of different devices: /device:TPU:18 before, /device:TPU:11 now
where the time goes in v2:
time: 273 us
  waiting for transfers between devices  90.2 us (33%)
  Pallas kernels  70.8 us (26%)
  matrix products  46.1 us (17%)
  starting transfers between devices  40 us (15%)
  other arithmetic  19 us (7%)
  local copies, waits for them, and re-layouts  5.67 us (2%)
    ppermute x18, waiting for transfers between devices, moved(): return lax.ppermute(value, axis, pairs)  90.2 us
    dot_general x4, matrix products, product(): lax.dot_general(left, right, (dims, ((), ())), preferred_element_type=jnp...  46.1 us
    ppermute x18, starting transfers between devices, moved(): return lax.ppermute(value, axis, pairs)  40 us
    pallas_call x2, Pallas kernels, packed_grad(): pl.pallas_call(functools.partial(grad_kernel, group=group, groups=groups,...  36.2 us
    pallas_call x2, Pallas kernels, unpack_half(): pl.pallas_call(functools.partial(unpack_half_kernel, cols=cols, capacity=...  20.2 us
    pallas_call x1, Pallas kernels, unpack(): pl.pallas_call(functools.partial(unpack_kernel, cols=cols, capacity=capac...  14.5 us
    convert_element_type x1, other arithmetic, body(): pre_grad = (hidden_grad * slope_of(pre)).astype(jnp.bfloat16)  7.1 us
  transfers between devices with their start and end apart: 18, of which 10 were waited for; matrix products, arithmetic and copies ran while one was open for 10% of the time, Pallas kernels for 26%

profile of v2, /device:TPU:11, one launch (start us, length us, event | category | flops | bytes accessed | tf_op | source)
XLA Modules:
  0.0 272.7 jit_solution(12265800127135715397)
XLA Ops:
  0.6 1.3 collective-permute-start
  1.9 0.8 reshape.44
  2.7 0.8 reshape_squeeze.6
  3.5 0.3 reduce-window.16
  3.8 0.1 slice.50
  3.9 0.1 slice_reduce_fusion.1
  4.0 0.7 fusion.3.slot_ref
  4.7 14.5 %unpack_tile.1 = bf16[32,2,32,3584]{3,2,1,0:T(8,128)(2,1)} custom-call(s32[1792]{0:T(1024)} %fusion.3.slot_ref, bf16[1024,4096]{1,0:T(8,128)(2,1)} %bitcast.37), custom_call_target="tpu_custom_call" | custom-call | tf_op jit(solution)/shard_map/unpack_tile/pallas_call | solution.py:81
  19.2 0.0 copy-start.6
  19.2 2.4 collective-permute-start.1
  21.6 0.1 copy.11
  21.6 0.1 reshape.47
  21.7 0.1 reshape_squeeze.7
  21.8 0.3 reduce-window.24
  22.1 0.1 slice.52
  22.2 0.1 slice_reduce_fusion
  22.3 0.7 fusion.2.slot_ref
  23.0 2.1 collective-permute-start.3
  25.1 3.2 %collective-permute-start.4 = (bf16[128,2048]{1,0:T(8,128)(2,1)S(1)}, bf16[128,2048]{1,0:T(8,128)(2,1)S(1)}, u32[]{:S(2)}, u32[]{:S(2)}) collective-permute-start(bf16[128,2048]{1,0:T(8,128)(2,1)S(1)} %bitcast.42), channel_id=1, source_target_pairs={{0,1},{1,2},{2,3},{4,5},{5,6},{6,7},{8,9},{9,10},{10,11},{12,13},{... | collective-permute-start | bytes 1572872 | tf_op jit(solution)/shard_map/ppermute | solution.py:283
  28.3 10.1 %unpack_half.2.refs_0_ = bf16[56,2,32,2048]{3,2,1,0:T(8,128)(2,1)} custom-call(s32[1792]{0:T(1024)} %fusion.2.slot_ref, bf16[1024,4096]{1,0:T(8,128)(2,1)} %bitcast.33), custom_call_target="tpu_custom_call" | custom-call | tf_op jit(solution)/shard_map/unpack_half/pallas_call | solution.py:159
  38.3 6.0 %collective-permute-done.1 = bf16[128,2048]{1,0:T(8,128)(2,1)} collective-permute-done((bf16[128,2048]{1,0:T(8,128)(2,1)S(1)}, bf16[128,2048]{1,0:T(8,128)(2,1)}, u32[]{:S(2)}, u32[]{:S(2)}) %collective-permute-start.1) | collective-permute-done | bytes 524320 | tf_op jit(solution)/shard_map/ppermute | solution.py:283
  44.4 2.1 collective-permute-start.2
  46.5 8.0 %collective-permute-done.3 = bf16[128,2048]{1,0:T(8,128)(2,1)S(1)} collective-permute-done((bf16[128,2048]{1,0:T(8,128)(2,1)S(1)}, bf16[128,2048]{1,0:T(8,128)(2,1)S(1)}, u32[]{:S(2)}, u32[]{:S(2)}) %collective-permute-start.3) | collective-permute-done | bytes 524320 | tf_op jit(solution)/shard_map/ppermute | solution.py:283
  54.5 1.1 collective-permute-done.4
  55.6 0.1 broadcast_select_fusion.3
  55.7 12.4 %convolution_convert_fusion.1 = bf16[512,3584]{1,0:T(8,128)(2,1)} fusion(bf16[2048,3584]{1,0:T(8,128)(2,1)} %bitcast.35, bf16[128,2048]{1,0:T(8,128)(2,1)S(1)} %get-tuple-element.31, bf16[128,2048]{1,0:T(8,128)(2,1)} %collective-permute-done.1, bf16[128,2048]{1,0:T(8,128)(2,1)S(1)} %get-tuple-element.30, bf16[128,2048]{1,0:T(8,128)(2,1)S(1)} %bitcast.43), kind=kOutput, calls=%fused_computation.5 | convolution fusion | flops 7526416384 | bytes 20447232 | tf_op jit(solution)/shard_map/dot_general | solution.py:314
  68.1 3.3 %collective-permute-start.5 = (bf16[512,3584]{1,0:T(8,128)(2,1)}, bf16[512,3584]{1,0:T(8,128)(2,1)}, u32[]{:S(2)}, u32[]{:S(2)}) collective-permute-start(bf16[512,3584]{1,0:T(8,128)(2,1)} %convolution_convert_fusion.1), channel_id=1, source_target_pairs={{0,4},{4,0},{1,5},{5,1},{2,6},{6,2},{3,7},{7,3},{8,12},{12,8},{9,1... | collective-permute-start | bytes 11010056 | tf_op jit(solution)/shard_map/ppermute | solution.py:283
  71.4 0.2 collective-permute-start.9
  71.6 10.1 %unpack_half.3 = bf16[56,2,32,2048]{3,2,1,0:T(8,128)(2,1)} custom-call(s32[1792]{0:T(1024)} %fusion.2.slot_ref, bf16[1024,4096]{1,0:T(8,128)(2,1)} %bitcast.34, bf16[56,2,32,2048]{3,2,1,0:T(8,128)(2,1)} %unpack_half.2.refs_0_), custom_call_target="tpu_custom_call", output_to_operand_aliasing={{}: (2, {})} | custom-call | tf_op jit(solution)/shard_map/unpack_half/pallas_call | solution.py:159
  81.7 4.0 %collective-permute-done.9 = bf16[1,128,2048]{2,1,0:T(8,128)(2,1)S(1)} collective-permute-done((bf16[1,128,2048]{2,1,0:T(8,128)(2,1)S(1)}, bf16[1,128,2048]{2,1,0:T(8,128)(2,1)S(1)}, u32[]{:S(2)}, u32[]{:S(2)}) %collective-permute-start.9) | collective-permute-done | bytes 524320 | tf_op jit(solution)/shard_map/ppermute | solution.py:283
  85.7 5.8 %collective-permute-start.10 = (bf16[128,2048]{1,0:T(8,128)(2,1)S(1)}, bf16[128,2048]{1,0:T(8,128)(2,1)S(1)}, u32[]{:S(2)}, u32[]{:S(2)}) collective-permute-start(bf16[128,2048]{1,0:T(8,128)(2,1)S(1)} %bitcast.45), channel_id=1, source_target_pairs={{0,2},{1,3},{2,0},{3,1},{4,6},{5,7},{6,4},{7,5},{8,10},{9,11},{10,... | collective-permute-start | bytes 1572872 | tf_op jit(solution)/shard_map/ppermute | solution.py:283
  91.5 1.9 collective-permute-start.12
  93.4 3.4 %collective-permute-start.13 = (bf16[128,2048]{1,0:T(8,128)(2,1)S(1)}, bf16[128,2048]{1,0:T(8,128)(2,1)S(1)}, u32[]{:S(2)}, u32[]{:S(2)}) collective-permute-start(bf16[128,2048]{1,0:T(8,128)(2,1)S(1)} %bitcast.47), channel_id=1, source_target_pairs={{0,1},{1,2},{2,3},{4,5},{5,6},{6,7},{8,9},{9,10},{10,11},{12,13},{... | collective-permute-start | bytes 1572872 | tf_op jit(solution)/shard_map/ppermute | solution.py:283
  96.8 16.7 %collective-permute-done.10 = bf16[128,2048]{1,0:T(8,128)(2,1)S(1)} collective-permute-done((bf16[128,2048]{1,0:T(8,128)(2,1)S(1)}, bf16[128,2048]{1,0:T(8,128)(2,1)S(1)}, u32[]{:S(2)}, u32[]{:S(2)}) %collective-permute-start.10) | collective-permute-done | bytes 524320 | tf_op jit(solution)/shard_map/ppermute | solution.py:283
  113.5 2.1 collective-permute-start.11
  115.6 7.9 %collective-permute-done.12 = bf16[128,2048]{1,0:T(8,128)(2,1)S(1)} collective-permute-done((bf16[128,2048]{1,0:T(8,128)(2,1)S(1)}, bf16[128,2048]{1,0:T(8,128)(2,1)S(1)}, u32[]{:S(2)}, u32[]{:S(2)}) %collective-permute-start.12) | collective-permute-done | bytes 524320 | tf_op jit(solution)/shard_map/ppermute | solution.py:283
  123.6 1.2 collective-permute-done.13
  124.7 0.1 broadcast_select_fusion.2
  124.8 0.1 pad_maximum_fusion.1.rhs_ref
  125.0 4.3 %multiply_convert_fusion.1.lhs_ref = bf16[512,3584]{1,0:T(8,128)(2,1)S(1)} fusion(bf16[512,3584]{1,0:T(8,128)(2,1)} %collective-permute-done.5, bf16[512,3584]{1,0:T(8,128)(2,1)} %convolution_convert_fusion.1), kind=kLoop, calls=%fused_computation.1 | loop fusion | flops 14680064 | bytes 11010048 | tf_op jit(solution)/shard_map/convert_element_type | solution.py:367
  129.4 2.8 %copy-done.2 = bf16[56,2,32,2048]{3,2,1,0:T(8,128)(2,1)S(1)} copy-done((bf16[56,2,32,2048]{3,2,1,0:T(8,128)(2,1)S(1)}, bf16[56,2,32,2048]{3,2,1,0:T(8,128)(2,1)}, u32[]{:S(2)}) %copy-start.2) | copy-done | bytes 14680088
  132.2 9.0 %convolution_convert_fusion.3 = bf16[512,2048]{1,0:T(8,128)(2,1)} fusion(bf16[512,3584]{1,0:T(8,128)(2,1)S(1)} %multiply_convert_fusion.1.lhs_ref, bf16[3584,2048]{1,0:T(8,128)(2,1)S(1)} %bitcast.32), kind=kOutput, calls=%fused_computation.7 | convolution fusion | flops 7517241344 | bytes 20447232 | tf_op jit(solution)/shard_map/dot_general | solution.py:314
  141.2 12.3 %convolution_convert_fusion = bf16[512,3584]{1,0:T(8,128)(2,1)} fusion(bf16[512,2048]{1,0:T(8,128)(2,1)S(1)} %pad_maximum_fusion.1.rhs_ref, bf16[3584,2048]{1,0:T(8,128)(2,1)} %bitcast.31), kind=kOutput, calls=%fused_computation.4 | convolution fusion | flops 7518027776 | bytes 20447232 | tf_op jit(solution)/shard_map/dot_general | solution.py:314
  153.5 2.8 %collective-permute-start.14 = (bf16[512,3584]{1,0:T(8,128)(2,1)}, bf16[512,3584]{1,0:T(8,128)(2,1)}, u32[]{:S(2)}, u32[]{:S(2)}) collective-permute-start(bf16[512,3584]{1,0:T(8,128)(2,1)} %convolution_convert_fusion), channel_id=1, source_target_pairs={{0,4},{4,0},{1,5},{5,1},{2,6},{6,2},{3,7},{7,3},{8,12},{12,8},{9,1... | collective-permute-start | bytes 11010056 | tf_op jit(solution)/shard_map/ppermute | solution.py:283
  156.3 0.6 reduce_sum.19
  157.0 0.7 reduce_sum.18
  157.6 1.5 pad_maximum_fusion.lhs_ref
  159.2 0.4 copy-done.5
  159.5 0.1 fusion.5
  159.6 3.8 %collective-permute-start.6 = (bf16[128,2048]{1,0:T(8,128)(2,1)S(1)}, bf16[128,2048]{1,0:T(8,128)(2,1)S(1)}, u32[]{:S(2)}, u32[]{:S(2)}) collective-permute-start(bf16[128,2048]{1,0:T(8,128)(2,1)S(1)} %get-tuple-element.25), channel_id=1, source_target_pairs={{0,1},{1,2},{2,3},{3,0},{4,5},{5,6},{6,7},{7,4},{8,9},{9,10},{10,1... | collective-permute-start | bytes 1572872 | tf_op jit(solution)/shard_map/ppermute | solution.py:283
  163.4 2.0 collective-permute-start.7
  165.4 1.4 collective-permute-start.8
  166.8 7.1 %multiply_convert_fusion.rhs_ref = bf16[512,3584]{1,0:T(8,128)(2,1)S(1)} fusion(bf16[512,3584]{1,0:T(8,128)(2,1)} %collective-permute-done.14, bf16[512,3584]{1,0:T(8,128)(2,1)} %convolution_convert_fusion, bf16[512,3584]{1,0:T(8,128)(2,1)} %collective-permute-done.5, bf16[512,3584]{1,0:T(8,128)(2,1)} %convolution_convert_fusion.1), kind=kLoop, calls=%fused_computation | loop fusion | flops 27525120 | bytes 18350080 | tf_op jit(solution)/shard_map/convert_element_type | solution.py:372
  173.9 12.4 %convolution_convert_fusion.2 = bf16[512,2048]{1,0:T(8,128)(2,1)S(1)} fusion(bf16[512,3584]{1,0:T(8,128)(2,1)S(1)} %multiply_convert_fusion.rhs_ref, bf16[2048,3584]{1,0:T(8,128)(2,1)} %bitcast.36), kind=kOutput, calls=%fused_computation.6 | convolution fusion | flops 7517241344 | bytes 20447232 | tf_op jit(solution)/shard_map/dot_general | solution.py:314
  186.4 0.1 fusion.4
  186.5 0.1 collective-permute-start.15
  186.6 2.2 collective-permute-start.16
  188.8 8.4 %collective-permute-done.6 = bf16[128,2048]{1,0:T(8,128)(2,1)S(1)} collective-permute-done((bf16[128,2048]{1,0:T(8,128)(2,1)S(1)}, bf16[128,2048]{1,0:T(8,128)(2,1)S(1)}, u32[]{:S(2)}, u32[]{:S(2)}) %collective-permute-start.6) | collective-permute-done | bytes 524320 | tf_op jit(solution)/shard_map/ppermute | solution.py:283
  197.2 33.7 %collective-permute-done.7 = bf16[128,2048]{1,0:T(8,128)(2,1)S(1)} collective-permute-done((bf16[128,2048]{1,0:T(8,128)(2,1)S(1)}, bf16[128,2048]{1,0:T(8,128)(2,1)S(1)}, u32[]{:S(2)}, u32[]{:S(2)}) %collective-permute-start.7) | collective-permute-done | bytes 524320 | tf_op jit(solution)/shard_map/ppermute | solution.py:283
  230.9 3.1 %collective-permute-done.8 = bf16[128,2048]{1,0:T(8,128)(2,1)S(1)} collective-permute-done((bf16[128,2048]{1,0:T(8,128)(2,1)S(1)}, bf16[128,2048]{1,0:T(8,128)(2,1)S(1)}, u32[]{:S(2)}, u32[]{:S(2)}) %collective-permute-start.8) | collective-permute-done | bytes 524320 | tf_op jit(solution)/shard_map/ppermute | solution.py:283
  234.0 1.2 fusion
  235.2 18.2 %packed_grad.2 = bf16[1024,4096]{1,0:T(8,128)(2,1)} custom-call(s32[1792]{0:T(1024)S(1)} %copy-done, s32[1]{0:T(128)} %bitcast.11.count_ref, bf16[512,3584]{1,0:T(8,128)(2,1)} %copy-done.3, bf16[512,2048]{1,0:T(8,128)(2,1)S(1)} %pad_maximum_fusion.1.rhs_ref), custom_call_target="tpu_custom_call" | custom-call | tf_op jit(solution)/shard_map/packed_grad/pallas_call | solution.py:256
  253.4 18.0 %packed_grad.3 = bf16[1024,4096]{1,0:T(8,128)(2,1)} custom-call(s32[1792]{0:T(1024)S(1)} %copy-done.1, s32[1]{0:T(128)} %bitcast.10.count_ref, bf16[512,2048]{1,0:T(8,128)(2,1)S(1)} %pad_maximum_fusion.lhs_ref, bf16[512,3584]{1,0:T(8,128)(2,1)} %copy-done.4), custom_call_target="tpu_custom_call" | custom-call | tf_op jit(solution)/shard_map/packed_grad/pallas_call | solution.py:256
  271.4 1.2 fusion.1
  (34 shorter events, 0.1 us)
Async XLA Ops:
  0.6 18.5 %collective-permute-start = (bf16[1,128,2048]{2,1,0:T(8,128)(2,1)}, bf16[1,128,2048]{2,1,0:T(8,128)(2,1)S(1)}, u32[]{:S(2)}, u32[]{:S(2)}) collective-permute-start(bf16[1,128,2048]{2,1,0:T(8,128)(2,1)} %param.6), channel_id=1, source_target_pairs={{0,8},{8,16},{16,24},{24,0},{1,9},{9,17},{17,25},{25,1},{2,10},{10... | collective-permute-start | bytes 1572872 | tf_op jit(solution)/shard_map/ppermute | solution.py:283
  4.7 16.9 %copy-start.11 = (s32[1,56,32]{1,2,0:T(8,128)S(1)}, s32[1,56,32]{1,2,0:T(8,128)}, u32[]{:S(2)}) copy-start(s32[1,56,32]{1,2,0:T(8,128)} %param.11) | copy-start | bytes 21508
  19.2 36.6 %copy-start.6 = (bf16[1,128,2048]{2,1,0:T(8,128)(2,1)}, bf16[1,128,2048]{2,1,0:T(8,128)(2,1)S(1)}, u32[]{:S(2)}) copy-start(bf16[1,128,2048]{2,1,0:T(8,128)(2,1)S(1)} %collective-permute-done) | copy-start | bytes 1572868
  19.2 25.2 %collective-permute-start.1 = (bf16[128,2048]{1,0:T(8,128)(2,1)S(1)}, bf16[128,2048]{1,0:T(8,128)(2,1)}, u32[]{:S(2)}, u32[]{:S(2)}) collective-permute-start(bf16[128,2048]{1,0:T(8,128)(2,1)S(1)} %bitcast.40), channel_id=1, source_target_pairs={{0,2},{1,3},{2,0},{3,1},{4,6},{5,7},{6,4},{7,5},{8,10},{9,11},{10,... | collective-permute-start | bytes 1572872 | tf_op jit(solution)/shard_map/ppermute | solution.py:283
  23.0 31.5 %collective-permute-start.3 = (bf16[128,2048]{1,0:T(8,128)(2,1)S(1)}, bf16[128,2048]{1,0:T(8,128)(2,1)S(1)}, u32[]{:S(2)}, u32[]{:S(2)}) collective-permute-start(bf16[128,2048]{1,0:T(8,128)(2,1)S(1)} %bitcast.41), channel_id=1, source_target_pairs={{1,0},{2,1},{3,2},{5,4},{6,5},{7,6},{9,8},{10,9},{11,10},{13,12},{... | collective-permute-start | bytes 1572872 | tf_op jit(solution)/shard_map/ppermute | solution.py:283
  25.1 30.6 %collective-permute-start.4 = (bf16[128,2048]{1,0:T(8,128)(2,1)S(1)}, bf16[128,2048]{1,0:T(8,128)(2,1)S(1)}, u32[]{:S(2)}, u32[]{:S(2)}) collective-permute-start(bf16[128,2048]{1,0:T(8,128)(2,1)S(1)} %bitcast.42), channel_id=1, source_target_pairs={{0,1},{1,2},{2,3},{4,5},{5,6},{6,7},{8,9},{9,10},{10,11},{12,13},{... | collective-permute-start | bytes 1572872 | tf_op jit(solution)/shard_map/ppermute | solution.py:283
  44.4 11.2 %collective-permute-start.2 = (bf16[128,2048]{1,0:T(8,128)(2,1)}, bf16[128,2048]{1,0:T(8,128)(2,1)S(1)}, u32[]{:S(2)}, u32[]{:S(2)}) collective-permute-start(bf16[128,2048]{1,0:T(8,128)(2,1)} %collective-permute-done.1), channel_id=1, source_target_pairs={{1,0},{2,3},{5,4},{6,7},{9,8},{10,11},{13,12},{14,15},{17,16},{18,... | collective-permute-start | bytes 1572872 | tf_op jit(solution)/shard_map/ppermute | solution.py:283
  55.7 15.6 %copy-start.12 = (bf16[1,128,2048]{2,1,0:T(8,128)(2,1)S(1)}, bf16[1,128,2048]{2,1,0:T(8,128)(2,1)}, u32[]{:S(2)}) copy-start(bf16[1,128,2048]{2,1,0:T(8,128)(2,1)} %param.7) | copy-start | bytes 1572868
  68.1 56.9 %collective-permute-start.5 = (bf16[512,3584]{1,0:T(8,128)(2,1)}, bf16[512,3584]{1,0:T(8,128)(2,1)}, u32[]{:S(2)}, u32[]{:S(2)}) collective-permute-start(bf16[512,3584]{1,0:T(8,128)(2,1)} %convolution_convert_fusion.1), channel_id=1, source_target_pairs={{0,4},{4,0},{1,5},{5,1},{2,6},{6,2},{3,7},{7,3},{8,12},{12,8},{9,1... | collective-permute-start | bytes 11010056 | tf_op jit(solution)/shard_map/ppermute | solution.py:283
  71.4 14.3 %collective-permute-start.9 = (bf16[1,128,2048]{2,1,0:T(8,128)(2,1)S(1)}, bf16[1,128,2048]{2,1,0:T(8,128)(2,1)S(1)}, u32[]{:S(2)}, u32[]{:S(2)}) collective-permute-start(bf16[1,128,2048]{2,1,0:T(8,128)(2,1)S(1)} %copy-done.12), channel_id=1, source_target_pairs={{0,24},{8,0},{16,8},{24,16},{1,25},{9,1},{17,9},{25,17},{2,26},{10... | collective-permute-start | bytes 1572872 | tf_op jit(solution)/shard_map/ppermute | solution.py:283
  85.7 43.6 %copy-start.8 = (bf16[1,128,2048]{2,1,0:T(8,128)(2,1)}, bf16[1,128,2048]{2,1,0:T(8,128)(2,1)S(1)}, u32[]{:S(2)}) copy-start(bf16[1,128,2048]{2,1,0:T(8,128)(2,1)S(1)} %collective-permute-done.9) | copy-start | bytes 1572868
  85.7 27.8 %collective-permute-start.10 = (bf16[128,2048]{1,0:T(8,128)(2,1)S(1)}, bf16[128,2048]{1,0:T(8,128)(2,1)S(1)}, u32[]{:S(2)}, u32[]{:S(2)}) collective-permute-start(bf16[128,2048]{1,0:T(8,128)(2,1)S(1)} %bitcast.45), channel_id=1, source_target_pairs={{0,2},{1,3},{2,0},{3,1},{4,6},{5,7},{6,4},{7,5},{8,10},{9,11},{10,... | collective-permute-start | bytes 1572872 | tf_op jit(solution)/shard_map/ppermute | solution.py:283
  91.5 32.1 %collective-permute-start.12 = (bf16[128,2048]{1,0:T(8,128)(2,1)S(1)}, bf16[128,2048]{1,0:T(8,128)(2,1)S(1)}, u32[]{:S(2)}, u32[]{:S(2)}) collective-permute-start(bf16[128,2048]{1,0:T(8,128)(2,1)S(1)} %bitcast.46), channel_id=1, source_target_pairs={{1,0},{2,1},{3,2},{5,4},{6,5},{7,6},{9,8},{10,9},{11,10},{13,12},{... | collective-permute-start | bytes 1572872 | tf_op jit(solution)/shard_map/ppermute | solution.py:283
  93.4 31.3 %collective-permute-start.13 = (bf16[128,2048]{1,0:T(8,128)(2,1)S(1)}, bf16[128,2048]{1,0:T(8,128)(2,1)S(1)}, u32[]{:S(2)}, u32[]{:S(2)}) collective-permute-start(bf16[128,2048]{1,0:T(8,128)(2,1)S(1)} %bitcast.47), channel_id=1, source_target_pairs={{0,1},{1,2},{2,3},{4,5},{5,6},{6,7},{8,9},{9,10},{10,11},{12,13},{... | collective-permute-start | bytes 1572872 | tf_op jit(solution)/shard_map/ppermute | solution.py:283
  113.5 11.2 %collective-permute-start.11 = (bf16[128,2048]{1,0:T(8,128)(2,1)S(1)}, bf16[128,2048]{1,0:T(8,128)(2,1)S(1)}, u32[]{:S(2)}, u32[]{:S(2)}) collective-permute-start(bf16[128,2048]{1,0:T(8,128)(2,1)S(1)} %collective-permute-done.10), channel_id=1, source_target_pairs={{1,0},{2,3},{5,4},{6,7},{9,8},{10,11},{13,12},{14,15},{17,16},{18,... | collective-permute-start | bytes 1572872 | tf_op jit(solution)/shard_map/ppermute | solution.py:283
  124.8 7.3 %copy-start.2 = (bf16[56,2,32,2048]{3,2,1,0:T(8,128)(2,1)S(1)}, bf16[56,2,32,2048]{3,2,1,0:T(8,128)(2,1)}, u32[]{:S(2)}) copy-start(bf16[56,2,32,2048]{3,2,1,0:T(8,128)(2,1)} %unpack_half.3) | copy-start | bytes 44040196
  132.2 9.0 %copy-start.3 = (bf16[512,3584]{1,0:T(8,128)(2,1)}, bf16[512,3584]{1,0:T(8,128)(2,1)S(1)}, u32[]{:S(2)}) copy-start(bf16[512,3584]{1,0:T(8,128)(2,1)S(1)} %multiply_convert_fusion.1.lhs_ref) | copy-start | bytes 11010052
  141.2 15.8 %copy-start.10 = (s32[1,32,56]{2,1,0:T(8,128)S(1)}, s32[1,32,56]{2,1,0:T(8,128)}, u32[]{:S(2)}) copy-start(s32[1,32,56]{2,1,0:T(8,128)} %param.10) | copy-start | bytes 21508
  153.5 13.3 %collective-permute-start.14 = (bf16[512,3584]{1,0:T(8,128)(2,1)}, bf16[512,3584]{1,0:T(8,128)(2,1)}, u32[]{:S(2)}, u32[]{:S(2)}) collective-permute-start(bf16[512,3584]{1,0:T(8,128)(2,1)} %convolution_convert_fusion), channel_id=1, source_target_pairs={{0,4},{4,0},{1,5},{5,1},{2,6},{6,2},{3,7},{7,3},{8,12},{12,8},{9,1... | collective-permute-start | bytes 11010056 | tf_op jit(solution)/shard_map/ppermute | solution.py:283
  157.6 1.9 copy-start.5
  159.6 37.5 %collective-permute-start.6 = (bf16[128,2048]{1,0:T(8,128)(2,1)S(1)}, bf16[128,2048]{1,0:T(8,128)(2,1)S(1)}, u32[]{:S(2)}, u32[]{:S(2)}) collective-permute-start(bf16[128,2048]{1,0:T(8,128)(2,1)S(1)} %get-tuple-element.25), channel_id=1, source_target_pairs={{0,1},{1,2},{2,3},{3,0},{4,5},{5,6},{6,7},{7,4},{8,9},{9,10},{10,1... | collective-permute-start | bytes 1572872 | tf_op jit(solution)/shard_map/ppermute | solution.py:283
  163.4 67.5 %collective-permute-start.7 = (bf16[128,2048]{1,0:T(8,128)(2,1)S(1)}, bf16[128,2048]{1,0:T(8,128)(2,1)S(1)}, u32[]{:S(2)}, u32[]{:S(2)}) collective-permute-start(bf16[128,2048]{1,0:T(8,128)(2,1)S(1)} %get-tuple-element.27), channel_id=1, source_target_pairs={{0,2},{1,3},{2,0},{3,1},{4,6},{5,7},{6,4},{7,5},{8,10},{9,11},{10,... | collective-permute-start | bytes 1572872 | tf_op jit(solution)/shard_map/ppermute | solution.py:283
  165.4 68.6 %collective-permute-start.8 = (bf16[128,2048]{1,0:T(8,128)(2,1)S(1)}, bf16[128,2048]{1,0:T(8,128)(2,1)S(1)}, u32[]{:S(2)}, u32[]{:S(2)}) collective-permute-start(bf16[128,2048]{1,0:T(8,128)(2,1)S(1)} %get-tuple-element.26), channel_id=1, source_target_pairs={{0,3},{1,0},{2,1},{3,2},{4,7},{5,4},{6,5},{7,6},{8,11},{9,8},{10,9... | collective-permute-start | bytes 1572872 | tf_op jit(solution)/shard_map/ppermute | solution.py:283
  173.9 12.4 %copy-start.4 = (bf16[512,3584]{1,0:T(8,128)(2,1)}, bf16[512,3584]{1,0:T(8,128)(2,1)S(1)}, u32[]{:S(2)}) copy-start(bf16[512,3584]{1,0:T(8,128)(2,1)S(1)} %multiply_convert_fusion.rhs_ref) | copy-start | bytes 11010052
  173.9 60.1 %copy-start.7 = (bf16[1,128,2048]{2,1,0:T(8,128)(2,1)S(1)}, bf16[1,128,2048]{2,1,0:T(8,128)(2,1)}, u32[]{:S(2)}) copy-start(bf16[1,128,2048]{2,1,0:T(8,128)(2,1)} %copy-done.6) | copy-start | bytes 1572868
  186.4 48.9 %copy-start = (s32[1792]{0:T(1024)S(1)}, s32[1792]{0:T(1024)}, u32[]{:S(2)}) copy-start(s32[1792]{0:T(1024)} %fusion.2.slot_ref) | copy-start | bytes 21508
  186.5 84.9 %collective-permute-start.15 = (bf16[128,2048]{1,0:T(8,128)(2,1)S(1)}, bf16[128,2048]{1,0:T(8,128)(2,1)S(1)}, u32[]{:S(2)}, u32[]{:S(2)}) collective-permute-start(bf16[128,2048]{1,0:T(8,128)(2,1)S(1)} %get-tuple-element.22), channel_id=1, source_target_pairs={{0,1},{1,2},{2,3},{3,0},{4,5},{5,6},{6,7},{7,4},{8,9},{9,10},{10,1... | collective-permute-start | bytes 1572872 | tf_op jit(solution)/shard_map/ppermute | solution.py:283
  186.6 84.8 %collective-permute-start.16 = (bf16[128,2048]{1,0:T(8,128)(2,1)S(1)}, bf16[128,2048]{1,0:T(8,128)(2,1)S(1)}, u32[]{:S(2)}, u32[]{:S(2)}) collective-permute-start(bf16[128,2048]{1,0:T(8,128)(2,1)S(1)} %get-tuple-element.24), channel_id=1, source_target_pairs={{0,2},{1,3},{2,0},{3,1},{4,6},{5,7},{6,4},{7,5},{8,10},{9,11},{10,... | collective-permute-start | bytes 1572872 | tf_op jit(solution)/shard_map/ppermute | solution.py:283
  197.2 74.3 %collective-permute-start.17 = (bf16[128,2048]{1,0:T(8,128)(2,1)S(1)}, bf16[128,2048]{1,0:T(8,128)(2,1)S(1)}, u32[]{:S(2)}, u32[]{:S(2)}) collective-permute-start(bf16[128,2048]{1,0:T(8,128)(2,1)S(1)} %get-tuple-element.23), channel_id=1, source_target_pairs={{0,3},{1,0},{2,1},{3,2},{4,7},{5,4},{6,5},{7,6},{8,11},{9,8},{10,9... | collective-permute-start | bytes 1572872 | tf_op jit(solution)/shard_map/ppermute | solution.py:283
  235.2 18.2 %copy-start.1 = (s32[1792]{0:T(1024)S(1)}, s32[1792]{0:T(1024)}, u32[]{:S(2)}) copy-start(s32[1792]{0:T(1024)} %fusion.3.slot_ref) | copy-start | bytes 21508
  253.4 18.0 %copy-start.9 = (bf16[1,128,2048]{2,1,0:T(8,128)(2,1)S(1)}, bf16[1,128,2048]{2,1,0:T(8,128)(2,1)}, u32[]{:S(2)}) copy-start(bf16[1,128,2048]{2,1,0:T(8,128)(2,1)} %copy-done.8) | copy-start | bytes 1572868
